TPU v7x, 256 devices: a whole 4x4x8 slice. The times are simulated.
256 devices in a mesh: req: 4 (over y), blk: 32 (over z, x), head: 2 (over core).
Axes of the slice: x: 4, y: 4, z: 8, core: 2. Of those that a mesh axis runs over, the one named last changes fastest.
Arguments:
- queries: bfloat16 [65536, 3584], P(('req', 'blk'), 'head'), parts along dimension 0, may hold values from -32 to 32
- keys: bfloat16 [65536, 3584], P(('req', 'blk'), 'head'), parts along dimension 0, may hold values from -32 to 32
- values: bfloat16 [65536, 3584], P(('req', 'blk'), 'head'), parts along dimension 0, may hold values from -6 to 6
- segment_ids: int32 [65536], P(('req', 'blk')), parts along dimension 0, may hold values from 0 to 15, never falling along the last dimension, each value on 1 to 2048 neighbouring positions
- page_table: int32 [512], P(('req', 'blk')), parts along dimension 0, may hold values from 0 to 127, as said below
Outputs:
- attended: bfloat16 [65536, 3584], P(('req', 'blk'), 'head'), parts along dimension 0
- kv_cache: bfloat16 [512, 128, 2, 3584], P(('req', 'blk'), None, None, 'head'), parts along dimension 0
There are 4 independent parts, one for each index of `req`. A program takes and returns all parts, laid end to end along the dimension named above; each array names one. Nothing has to cross between parts.
Inputs may be any that keep to these rules, and one draw needn't show every extreme that they name: segment_ids never fall along the packed tokens and take every value 0 to 15; each prompt holds 1 to 2048 tokens, one exactly 2048. page_table names every cache slot exactly once; the pages of the packed block b (its 512 tokens) take, in a drawn order, the slots of the pages of block b + 4, counted around the group past the last block to the first.
All inputs are finite; a program needn't handle non-finite values.
Results may differ from a plain program's by a relative error of at most 0.0055.
Values may be sent and summed in bfloat16 or wider, within the bound.
No kernel may reach another device: no remote copies, remote signals or barrier semaphores. Data moves between devices by JAX's collectives and lax.ppermute only.
A program may use at most 128 MiB of HBM per device.

v0:
```python
import jax
import jax.numpy as jnp
from jax import lax
from jax.sharding import PartitionSpec as P

HD = 224
PAGE = 128


NEG = -1e30


def shifted(block, axis, distance):
    devices = range(lax.axis_size(axis))
    route = [((i - distance) % len(devices), i) for i in devices]
    return lax.ppermute(block, axis, route)


def per_device(queries, keys, values, segment_ids, page_table):
    count = queries.shape[0]
    width = queries.shape[1]
    heads = width // HD
    blocks = lax.axis_size("blk")
    reach = min(4, blocks - 1)
    index_self = lax.axis_index("blk")
    scale = (HD / 2.0) ** (-0.5)
    rows = jnp.arange(count, dtype=jnp.int32)
    own_pos = index_self * count + rows
    page_rows = rows // PAGE
    page_count = page_table.shape[0]
    pages_here = jnp.arange(page_count, dtype=jnp.int32)
    slot_page = jnp.sum(
        jnp.where(page_rows[:, None] == pages_here[None, :], page_table[None, :], 0), axis=1
    )
    token_slot = slot_page * PAGE + rows % PAGE
    tags = jnp.stack([segment_ids, token_slot], axis=1)
    pairs = jnp.stack([keys, values], axis=1)
    query_grid = queries.reshape(count, heads, HD)

    def update(state, piece, key_pos, key_seg):
        top, total, summed = state
        size = piece.shape[0]
        key_grid = piece[:, 0].reshape(size, heads, HD)
        value_grid = piece[:, 1].reshape(size, heads, HD)
        scores = (
            jnp.einsum("thd,uhd->htu", query_grid, key_grid, preferred_element_type=jnp.float32)
            * scale
        )
        allowed = (segment_ids[:, None] == key_seg[None, :]) & (
            key_pos[None, :] <= own_pos[:, None]
        )
        scores = jnp.where(allowed[None], scores, NEG)
        new_top = jnp.maximum(top, jnp.max(scores, axis=2))
        factor = jnp.exp(top - new_top)
        weights = jnp.where(allowed[None], jnp.exp(scores - new_top[:, :, None]), 0.0)
        new_total = total * factor + jnp.sum(weights, axis=2)
        term = jnp.einsum(
            "htu,uhd->thd",
            weights.astype(jnp.bfloat16),
            value_grid,
            preferred_element_type=jnp.float32,
        )
        new_summed = summed * jnp.repeat(factor.T, HD, axis=1) + term.reshape(count, width)
        return (new_top, new_total, new_summed)

    def step(state, piece, piece_tags, start):
        size = piece.shape[0]
        key_pos = start + jnp.arange(size, dtype=jnp.int32)
        key_seg = piece_tags[:, 0]
        return update(state, piece, key_pos, key_seg)

    start_state = (
        jnp.full((heads, count), NEG, jnp.float32),
        jnp.zeros((heads, count), jnp.float32),
        jnp.zeros((count, width), jnp.float32),
    )
    state = step(start_state, pairs, tags, index_self * count)

    def turn_one(index, carry):
        inner, ahead = carry
        ahead = shifted((ahead[0], ahead[1]), "blk", 1)
        inner = step(inner, ahead[0], ahead[1], (index_self - index) % blocks * count)
        return (inner, ahead)

    state, last_block = lax.fori_loop(1, reach + 1, turn_one, (state, (pairs, tags)))
    arrived_slots = (
        last_block[1].reshape(page_count, PAGE, 2)[:, 0, 1] // PAGE - index_self * page_count
    )
    selector = (pages_here[:, None] == arrived_slots[None, :]).astype(jnp.bfloat16)
    page_block = last_block[0].reshape(page_count, PAGE * 2 * width)
    placed = jnp.dot(selector, page_block, preferred_element_type=jnp.float32)
    cache = placed.astype(jnp.bfloat16).reshape(page_count, PAGE, 2, width)
    top, total, summed = state
    mixed = (summed / jnp.repeat(total.T, HD, axis=1)).astype(jnp.bfloat16)
    return (mixed, cache)


def solution(mesh):
    in_specs = (
        P(("req", "blk"), "head"),
        P(("req", "blk"), "head"),
        P(("req", "blk"), "head"),
        P(("req", "blk")),
        P(("req", "blk")),
    )
    out_specs = (P(("req", "blk"), "head"), P(("req", "blk"), None, None, "head"))
    return jax.shard_map(
        per_device, mesh=mesh, in_specs=in_specs, out_specs=out_specs, check_vma=False
    )
```

profile of v0, /device:TPU:16, one launch (start us, length us, event | category | flops | bytes accessed | tf_op | source)
XLA Modules:
  0.0 466.5 jit_solution(12608150939391743794)
XLA Ops:
  1.7 3.8 copy.28
  5.5 2.8 copy.29
  8.3 3.2 fusion.16
  14.8 3.9 copy.30
  18.6 8.5 %bitcast_add_fusion.1 = f32[512,8,224]{0,2,1:T(8,128)} fusion(bf16[512,8,224]{0,2,1:T(8,128)(2,1)} %bitcast.72, f32[8,512,512]{1,2,0:T(8,128)} %copy-done.2, f32[8,512]{1,0:T(8,128)S(1)} %broadcast_maximum_fusion, pred[512,512]{0,1:T(8,128)(4,1)S(1)} %compare_and_fusion.1, f32[512,8]{0,1:T(8,128)S(1)} %get-tuple-element.307), kind=kOutput, calls=%fused_computation.38 | convolution fusion | flops 950927360 | bytes 14188544 | tf_op jit(solution)/shard_map/htu,uhd->thd/dot_general | solution.py:57
  29.5 402.5 %while.24 = (s32[]{:T(128)}, f32[8,512]{1,0:T(8,128)S(1)}, f32[8,512]{1,0:T(8,128)S(1)}, f32[512,1792]{0,1:T(8,128)}, bf16[512,2,1792]{0,2,1:T(8,128)(2,1)}, /*i...) while((s32[]{:T(128)}, f32[8,512]{1,0:T(8,128)S(1)}, ...), condition=%wide.region_6.7_spmd.clone, body=%wide.region_3.6_spmd.clone.sunk | while | flops 1908945920 | bytes 112763320 | solution.py:85
  32.7 84.8 %collective-permute-done = s32[512,2]{0,1:T(2,128)S(1)} collective-permute-done((s32[512,2]{0,1:T(2,128)S(1)}, s32[512,2]{0,1:T(2,128)S(1)}, u32[]{:S(2)}, u32[]{:S(2)}) %collective-permute-start) | collective-permute-done | bytes 4128 | tf_op jit(solution)/shard_map/while/body/eval_jaxpr/ppermute | solution.py:16
  124.2 2.7 fusion.65
  128.1 5.4 %copy.56 = bf16[512,2,1792]{0,2,1:T(8,128)(2,1)} copy(bf16[512,2,1792]{0,2,1:T(8,128)(2,1)} %collective-permute-done.1) | data formatting | bytes 7340032 | tf_op jit(solution)/shard_map/while
  133.6 84.2 %collective-permute-done = s32[512,2]{0,1:T(2,128)S(1)} collective-permute-done((s32[512,2]{0,1:T(2,128)S(1)}, s32[512,2]{0,1:T(2,128)S(1)}, u32[]{:S(2)}, u32[]{:S(2)}) %collective-permute-start) | collective-permute-done | bytes 4128 | tf_op jit(solution)/shard_map/while/body/eval_jaxpr/ppermute | solution.py:16
  218.1 2.4 fusion.61
  224.5 2.7 fusion.65
  228.5 5.4 %copy.56 = bf16[512,2,1792]{0,2,1:T(8,128)(2,1)} copy(bf16[512,2,1792]{0,2,1:T(8,128)(2,1)} %collective-permute-done.1) | data formatting | bytes 7340032 | tf_op jit(solution)/shard_map/while
  234.0 83.3 %collective-permute-done = s32[512,2]{0,1:T(2,128)S(1)} collective-permute-done((s32[512,2]{0,1:T(2,128)S(1)}, s32[512,2]{0,1:T(2,128)S(1)}, u32[]{:S(2)}, u32[]{:S(2)}) %collective-permute-start) | collective-permute-done | bytes 4128 | tf_op jit(solution)/shard_map/while/body/eval_jaxpr/ppermute | solution.py:16
  324.0 2.7 fusion.65
  327.9 5.4 %copy.56 = bf16[512,2,1792]{0,2,1:T(8,128)(2,1)} copy(bf16[512,2,1792]{0,2,1:T(8,128)(2,1)} %collective-permute-done.1) | data formatting | bytes 7340032 | tf_op jit(solution)/shard_map/while
  333.4 82.4 %collective-permute-done = s32[512,2]{0,1:T(2,128)S(1)} collective-permute-done((s32[512,2]{0,1:T(2,128)S(1)}, s32[512,2]{0,1:T(2,128)S(1)}, u32[]{:S(2)}, u32[]{:S(2)}) %collective-permute-start) | collective-permute-done | bytes 4128 | tf_op jit(solution)/shard_map/while/body/eval_jaxpr/ppermute | solution.py:16
  422.6 2.7 fusion.65
  426.5 5.4 %copy.56 = bf16[512,2,1792]{0,2,1:T(8,128)(2,1)} copy(bf16[512,2,1792]{0,2,1:T(8,128)(2,1)} %collective-permute-done.1) | data formatting | bytes 7340032 | tf_op jit(solution)/shard_map/while
  431.9 2.5 fusion.26
  436.8 9.9 %copy.35 = bf16[512,2,1792]{2,1,0:T(2,128)(2,1)} copy(bf16[512,2,1792]{0,2,1:T(8,128)(2,1)} %get-tuple-element.251) | data formatting | bytes 7340032 | tf_op jit(solution)/shard_map/while | solution.py:85
  446.7 6.1 %reshape.262 = bf16[4,458752]{1,0:T(4,128)(2,1)} reshape(bf16[512,2,1792]{2,1,0:T(2,128)(2,1)} %copy.35) | data formatting | bytes 7340032 | tf_op jit(solution)/shard_map/reshape | solution.py:90
  453.0 5.9 %convolution_convert_fusion = bf16[4,458752]{1,0:T(4,128)(2,1)} fusion(bf16[4,458752]{1,0:T(4,128)(2,1)} %reshape.262, s32[4]{0:T(128)S(1)} %fusion.36), kind=kOutput, calls=%fused_computation.23 | convolution fusion | flops 16515088 | bytes 7340048 | tf_op jit(solution)/shard_map/dot_general | solution.py:91
  458.9 7.5 %reshape.263 = bf16[4,128,2,1792]{3,2,1,0:T(2,128)(2,1)} reshape(bf16[4,458752]{1,0:T(4,128)(2,1)} %convolution_convert_fusion) | data formatting | bytes 7340032 | tf_op jit(solution)/shard_map/reshape | solution.py:92
  (103 shorter events, 41.2 us)
Async XLA Ops:
  11.5 3.2 copy-start.2
  18.6 8.6 %copy-start.3 = (bf16[512,1792]{0,1:T(8,128)(2,1)S(1)}, bf16[512,1792]{0,1:T(8,128)(2,1)}, u32[]{:S(2)}) copy-start(bf16[512,1792]{0,1:T(8,128)(2,1)} %copy.30) | copy-start | bytes 5505028
  27.2 2.2 copy-start.6
  27.2 2.3 copy-start.5
  29.7 88.1 %collective-permute-start.1 = (bf16[512,2,1792]{0,2,1:T(8,128)(2,1)}, bf16[512,2,1792]{0,2,1:T(8,128)(2,1)}, u32[]{:S(2)}, u32[]{:S(2)}) collective-permute-start(bf16[512,2,1792]{0,2,1:T(8,128)(2,1)} %get-tuple-element.407), channel_id=1, source_target_pairs={{62,0},{0,2},{2,4},{4,6},{6,8},{8,10},{10,12},{12,14},{14,16},{16,... | collective-permute-start | bytes 11010056 | tf_op jit(solution)/shard_map/while/body/eval_jaxpr/ppermute | solution.py:16
  31.2 86.2 %collective-permute-start = (s32[512,2]{0,1:T(2,128)S(1)}, s32[512,2]{0,1:T(2,128)S(1)}, u32[]{:S(2)}, u32[]{:S(2)}) collective-permute-start(s32[512,2]{0,1:T(2,128)S(1)} %get-tuple-element.408), channel_id=1, source_target_pairs={{62,0},{0,2},{2,4},{4,6},{6,8},{8,10},{10,12},{12,14},{14,16},{16,... | collective-permute-start | bytes 12296 | tf_op jit(solution)/shard_map/while/body/eval_jaxpr/ppermute | solution.py:16
  117.8 2.6 copy-start.4
  124.2 2.7 copy-start
  128.1 5.5 %copy-start.1 = (f32[512,1792]{0,1:T(8,128)}, f32[512,1792]{0,1:T(8,128)S(1)}, u32[]{:S(2)}) copy-start(f32[512,1792]{0,1:T(8,128)S(1)} %bitcast_add_fusion.3) | copy-start | bytes 11010052 | tf_op jit(solution)/shard_map/while
  133.6 84.5 %collective-permute-start.1 = (bf16[512,2,1792]{0,2,1:T(8,128)(2,1)}, bf16[512,2,1792]{0,2,1:T(8,128)(2,1)}, u32[]{:S(2)}, u32[]{:S(2)}) collective-permute-start(bf16[512,2,1792]{0,2,1:T(8,128)(2,1)} %get-tuple-element.407), channel_id=1, source_target_pairs={{62,0},{0,2},{2,4},{4,6},{6,8},{8,10},{10,12},{12,14},{14,16},{16,... | collective-permute-start | bytes 11010056 | tf_op jit(solution)/shard_map/while/body/eval_jaxpr/ppermute | solution.py:16
  133.6 84.2 %collective-permute-start = (s32[512,2]{0,1:T(2,128)S(1)}, s32[512,2]{0,1:T(2,128)S(1)}, u32[]{:S(2)}, u32[]{:S(2)}) collective-permute-start(s32[512,2]{0,1:T(2,128)S(1)} %get-tuple-element.408), channel_id=1, source_target_pairs={{62,0},{0,2},{2,4},{4,6},{6,8},{8,10},{10,12},{12,14},{14,16},{16,... | collective-permute-start | bytes 12296 | tf_op jit(solution)/shard_map/while/body/eval_jaxpr/ppermute | solution.py:16
  218.1 2.6 copy-start.4
  224.5 2.7 copy-start
  228.5 5.5 %copy-start.1 = (f32[512,1792]{0,1:T(8,128)}, f32[512,1792]{0,1:T(8,128)S(1)}, u32[]{:S(2)}) copy-start(f32[512,1792]{0,1:T(8,128)S(1)} %bitcast_add_fusion.3) | copy-start | bytes 11010052 | tf_op jit(solution)/shard_map/while
  233.9 83.7 %collective-permute-start.1 = (bf16[512,2,1792]{0,2,1:T(8,128)(2,1)}, bf16[512,2,1792]{0,2,1:T(8,128)(2,1)}, u32[]{:S(2)}, u32[]{:S(2)}) collective-permute-start(bf16[512,2,1792]{0,2,1:T(8,128)(2,1)} %get-tuple-element.407), channel_id=1, source_target_pairs={{62,0},{0,2},{2,4},{4,6},{6,8},{8,10},{10,12},{12,14},{14,16},{16,... | collective-permute-start | bytes 11010056 | tf_op jit(solution)/shard_map/while/body/eval_jaxpr/ppermute | solution.py:16
  233.9 83.4 %collective-permute-start = (s32[512,2]{0,1:T(2,128)S(1)}, s32[512,2]{0,1:T(2,128)S(1)}, u32[]{:S(2)}, u32[]{:S(2)}) collective-permute-start(s32[512,2]{0,1:T(2,128)S(1)} %get-tuple-element.408), channel_id=1, source_target_pairs={{62,0},{0,2},{2,4},{4,6},{6,8},{8,10},{10,12},{12,14},{14,16},{16,... | collective-permute-start | bytes 12296 | tf_op jit(solution)/shard_map/while/body/eval_jaxpr/ppermute | solution.py:16
  317.6 2.6 copy-start.4
  324.0 2.7 copy-start
  327.9 5.5 %copy-start.1 = (f32[512,1792]{0,1:T(8,128)}, f32[512,1792]{0,1:T(8,128)S(1)}, u32[]{:S(2)}) copy-start(f32[512,1792]{0,1:T(8,128)S(1)} %bitcast_add_fusion.3) | copy-start | bytes 11010052 | tf_op jit(solution)/shard_map/while
  333.4 82.8 %collective-permute-start.1 = (bf16[512,2,1792]{0,2,1:T(8,128)(2,1)}, bf16[512,2,1792]{0,2,1:T(8,128)(2,1)}, u32[]{:S(2)}, u32[]{:S(2)}) collective-permute-start(bf16[512,2,1792]{0,2,1:T(8,128)(2,1)} %get-tuple-element.407), channel_id=1, source_target_pairs={{62,0},{0,2},{2,4},{4,6},{6,8},{8,10},{10,12},{12,14},{14,16},{16,... | collective-permute-start | bytes 11010056 | tf_op jit(solution)/shard_map/while/body/eval_jaxpr/ppermute | solution.py:16
  333.4 82.5 %collective-permute-start = (s32[512,2]{0,1:T(2,128)S(1)}, s32[512,2]{0,1:T(2,128)S(1)}, u32[]{:S(2)}, u32[]{:S(2)}) collective-permute-start(s32[512,2]{0,1:T(2,128)S(1)} %get-tuple-element.408), channel_id=1, source_target_pairs={{62,0},{0,2},{2,4},{4,6},{6,8},{8,10},{10,12},{12,14},{14,16},{16,... | collective-permute-start | bytes 12296 | tf_op jit(solution)/shard_map/while/body/eval_jaxpr/ppermute | solution.py:16
  416.1 2.6 copy-start.4
  422.6 2.7 copy-start
  426.5 5.5 %copy-start.1 = (f32[512,1792]{0,1:T(8,128)}, f32[512,1792]{0,1:T(8,128)S(1)}, u32[]{:S(2)}) copy-start(f32[512,1792]{0,1:T(8,128)S(1)} %bitcast_add_fusion.3) | copy-start | bytes 11010052 | tf_op jit(solution)/shard_map/while
where the time goes:
time: 467 us; the launch traced here: 466 us
  waiting for transfers between devices  335 us (72%)
  local copies, waits for them, and re-layouts  70 us (15%)
  matrix products  35.3 us (8%)
  other arithmetic  22 us (5%)
    ppermute x8, waiting for transfers between devices, shifted(): return lax.ppermute(block, axis, route)  335 us
    while x36, local copies, waits for them, and re-layouts  22.5 us
    dot_general x5, matrix products, update(): jnp.einsum('htu,uhd->thd', weights.astype(jnp.bfloat16), value_grid, pref...  19.3 us
    unnamed x13, local copies, waits for them, and re-layouts  14.2 us
    reduce_sum x5, other arithmetic, update(): new_total = total * factor + jnp.sum(weights, axis=2)  10.2 us
    dot_general x5, matrix products, update(): jnp.einsum('thd,uhd->htu', query_grid, key_grid, preferred_element_type=j...  10.1 us
    while x1, local copies, waits for them, and re-layouts, per_device(): lax.fori_loop(1, reach + 1, turn_one, (state, (pairs, tags)))  9.92 us
    slice x4, local copies, waits for them, and re-layouts, update(): value_grid = piece[:, 1].reshape(size, heads, HD)  9.68 us
  transfers between devices with their start and end apart: 8, of which 4 were waited for; matrix products, arithmetic and copies ran while one was open for 0% of the time, Pallas kernels for 0%

commit v1 on v0

v1 whole, which is shorter than its diff:
```python
import jax
import jax.numpy as jnp
from jax import lax
from jax.experimental import pallas as pl
from jax.experimental.pallas import tpu as pltpu
from jax.sharding import PartitionSpec as P

HD = 224
PAGE = 128
NSEG = 16
COLS = 4
SLAB = COLS * HD
WIDE = 256
TQ = 256
TK = 512
NEG = -1e30
SCALE_LOG2 = (HD / 2.0) ** (-0.5) * 1.4426950408889634

VMEM = pl.BlockSpec(memory_space=pltpu.VMEM)
SMEM = pl.BlockSpec(memory_space=pltpu.SMEM)


def params():
    return pltpu.CompilerParams(vmem_limit_bytes=48 * 1024 * 1024)


def regroup(parts):
    return [
        jnp.concatenate([part[:, b * HD : (b + 1) * HD] for part in parts], axis=1)
        for b in range(COLS)
    ]


def pack_kernel(col_ref, q_ref, k_ref, v_ref, own, one, two, three, zrow, zlate, held):
    col = col_ref[0]
    outs = (own, one, two, three)
    for t, ref in enumerate((q_ref, k_ref, v_ref)):
        pages = [ref[p * PAGE : (p + 1) * PAGE, :] for p in range(COLS)]
        for j, piece in enumerate(regroup(pages)):
            held[t, j] = piece
    for r in range(COLS):
        slot = lax.rem(col + r, COLS)
        for t in range(3):
            outs[r][t] = held[t, slot]
        for t in range(2):
            if r == 2:
                zlate[t] = held[t + 1, slot]
            else:
                zrow[(0, 1, None, 2)[r], t] = held[t + 1, slot]


def pack(col, queries, keys, values, half):
    block = pl.BlockSpec((COLS * PAGE, SLAB), lambda i: (0, half))
    piece = jax.ShapeDtypeStruct((3, PAGE, SLAB), jnp.bfloat16)
    return pl.pallas_call(
        pack_kernel,
        grid=(1,),
        out_shape=[piece] * 4
        + [
            jax.ShapeDtypeStruct((3, 2, PAGE, SLAB), jnp.bfloat16),
            jax.ShapeDtypeStruct((2, PAGE, SLAB), jnp.bfloat16),
        ],
        in_specs=[SMEM, block, block, block],
        out_specs=[VMEM] * 6,
        scratch_shapes=[pltpu.VMEM((3, COLS, PAGE, SLAB), jnp.bfloat16)],
        compiler_params=params(),
        name="pack",
        cost_estimate=pl.CostEstimate(flops=0, transcendentals=0, bytes_accessed=6 * 1024 * 1024),
    )(col, queries, keys, values)


def attend_kernel(
    col_ref, start_smem, start_ref, a0, a1, a2, a3, zrow, p1, p2, p3,
    o0, o1, o2, o3, qs, ks, vs, os, m_ref, acc_ref,
):
    col = col_ref[0]
    rows = COLS * PAGE
    zeros = jnp.zeros((PAGE, WIDE - HD), jnp.bfloat16)
    ones = jnp.ones((PAGE, WIDE - HD), jnp.bfloat16)

    def spread(dst, base, piece, fill):
        for p in range(COLS):
            at = pl.multiple_of(base + p * PAGE, PAGE)
            dst[pl.ds(at, PAGE), :] = jnp.concatenate(
                [piece[:, p * HD : (p + 1) * HD], fill], axis=1
            )

    for r, ref in enumerate((a0, a1, a2, a3)):
        base = lax.rem(col - r + COLS, COLS) * rows
        spread(qs, base, ref[0], zeros)
        spread(ks, base + COLS * rows, ref[1], zeros)
        spread(vs, base + COLS * rows, ref[2], ones)
    for r, ref in enumerate((zrow.at[0], p1, p2, p3)):
        base = lax.rem(col - r + COLS, COLS) * rows
        spread(ks, base, ref[0], zeros)
        spread(vs, base, ref[1], ones)

    per = rows // TQ

    def query_tile(i, _):
        c = lax.div(i, per)
        r = lax.rem(col - c + COLS, COLS)
        off = pl.multiple_of(lax.rem(i, per) * TQ, TQ)
        qb = pl.multiple_of(i * TQ, TQ)
        t0 = COLS * rows + qb
        s_first = start_smem[r * rows + off]
        s_last = start_smem[r * rows + off + TQ - 1]
        m_ref[...] = jnp.full_like(m_ref, NEG)
        acc_ref[...] = jnp.zeros_like(acc_ref)

        def tile(kb, masked):
            s = lax.dot_general(
                qs[pl.ds(qb, TQ), :], ks[pl.ds(kb, TK), :],
                (((1,), (1,)), ((), ())), preferred_element_type=jnp.float32,
            )
            if masked:
                u = kb + lax.broadcasted_iota(jnp.int32, (TQ, TK), 1)
                t = t0 + lax.broadcasted_iota(jnp.int32, (TQ, TK), 0)
                first = jnp.tile(start_ref[r, pl.ds(off, TQ), :], (1, TK // 128))
                s = jnp.where((u >= first) & (u <= t), s, NEG)
            m_old = m_ref[...]
            m_new = jnp.maximum(m_old, jnp.max(s, axis=1, keepdims=True))
            m_ref[...] = m_new
            fade = jnp.exp2((m_old - m_new) * SCALE_LOG2)
            w = jnp.exp2((s - jnp.tile(m_new, (1, TK // 128))) * SCALE_LOG2)
            acc_ref[...] = acc_ref[...] * jnp.tile(fade, (1, WIDE // 128)) + jnp.dot(
                w.astype(jnp.bfloat16), vs[pl.ds(kb, TK), :], preferred_element_type=jnp.float32
            )

        def key_tile(kk, _):
            kb = pl.multiple_of(kk * TK, TK)
            full = (kb >= s_last) & (kb + TK - 1 <= t0)

            @pl.when(full)
            def _():
                tile(kb, False)

            @pl.when(jnp.logical_not(full))
            def _():
                tile(kb, True)

            return 0

        lax.fori_loop(lax.div(s_first, TK), lax.div(t0 + TQ - 1, TK) + 1, key_tile, 0)
        total = acc_ref[...]
        os[pl.ds(qb, TQ), :] = (total / total[:, HD : HD + 1]).astype(jnp.bfloat16)
        return 0

    lax.fori_loop(0, COLS * per, query_tile, 0)
    for r, out in enumerate((o0, o1, o2, o3)):
        base = lax.rem(col + r, COLS) * rows
        out[...] = jnp.concatenate(
            [os[pl.ds(pl.multiple_of(base + p * PAGE, PAGE), PAGE), :][:, :HD] for p in range(COLS)],
            axis=1,
        )


def attend(col, start_flat, start_wide, own, zrow, prior):
    rows = COLS * PAGE
    total = COLS * rows
    piece = jax.ShapeDtypeStruct((PAGE, SLAB), jnp.bfloat16)
    return pl.pallas_call(
        attend_kernel,
        out_shape=[piece] * 4,
        in_specs=[SMEM, SMEM] + [VMEM] * 9,
        out_specs=[VMEM] * 4,
        scratch_shapes=[
            pltpu.VMEM((total, WIDE), jnp.bfloat16),
            pltpu.VMEM((2 * total, WIDE), jnp.bfloat16),
            pltpu.VMEM((2 * total, WIDE), jnp.bfloat16),
            pltpu.VMEM((total, WIDE), jnp.bfloat16),
            pltpu.VMEM((TQ, 128), jnp.float32),
            pltpu.VMEM((TQ, WIDE), jnp.float32),
        ],
        compiler_params=params(),
        name="attend",
        cost_estimate=pl.CostEstimate(
            flops=4 * total * total * WIDE, transcendentals=total * total, bytes_accessed=6 * 1024 * 1024
        ),
    )(col, start_flat, start_wide, *own, zrow, *prior)


def unpack_kernel(col_ref, *refs):
    col = col_ref[0]
    out, held = refs[8], refs[9]
    for half in range(2):
        for r in range(COLS):
            held[half, lax.rem(col - r + COLS, COLS)] = refs[half * COLS + r][...]
        parts = [held[half, j] for j in range(COLS)]
        for p, page in enumerate(regroup(parts)):
            out[p * PAGE : (p + 1) * PAGE, half * SLAB : (half + 1) * SLAB] = page


def unpack(col, pieces):
    return pl.pallas_call(
        unpack_kernel,
        out_shape=jax.ShapeDtypeStruct((COLS * PAGE, 2 * SLAB), jnp.bfloat16),
        in_specs=[SMEM] + [VMEM] * 8,
        out_specs=VMEM,
        scratch_shapes=[pltpu.VMEM((2, COLS, PAGE, SLAB), jnp.bfloat16)],
        compiler_params=params(),
        name="unpack",
        cost_estimate=pl.CostEstimate(flops=0, transcendentals=0, bytes_accessed=4 * 1024 * 1024),
    )(col, *pieces)


def cache_kernel(col_ref, slot_ref, zrow_a, zlate_a, zrow_b, zlate_b, out, held):
    col = col_ref[0]
    for half, (zrow, zlate) in enumerate(((zrow_a, zlate_a), (zrow_b, zlate_b))):
        for r in range(COLS):
            at = lax.rem(col + r, COLS)
            for t in range(2):
                held[t, at] = zlate[t] if r == 2 else zrow[(0, 1, None, 2)[r], t]
        for t in range(2):
            parts = [held[t, j] for j in range(COLS)]
            for p, page in enumerate(regroup(parts)):
                out[slot_ref[p], :, t, half * SLAB : (half + 1) * SLAB] = page


def cache(col, slots, zrow_a, zlate_a, zrow_b, zlate_b):
    return pl.pallas_call(
        cache_kernel,
        out_shape=jax.ShapeDtypeStruct((COLS, PAGE, 2, 2 * SLAB), jnp.bfloat16),
        in_specs=[SMEM, SMEM] + [VMEM] * 4,
        out_specs=VMEM,
        scratch_shapes=[pltpu.VMEM((2, COLS, PAGE, SLAB), jnp.bfloat16)],
        compiler_params=params(),
        name="cache",
        cost_estimate=pl.CostEstimate(flops=0, transcendentals=0, bytes_accessed=8 * 1024 * 1024),
    )(col, slots, zrow_a, zlate_a, zrow_b, zlate_b)


def per_device(queries, keys, values, segment_ids, page_table):
    blocks = lax.axis_size("blk")
    index = lax.axis_index("blk")
    col = lax.rem(index, COLS).astype(jnp.int32).reshape(1)
    count = queries.shape[0]
    pages = page_table.shape[0]

    def across(value, r):
        route = [(i, i - i % COLS + (i % COLS + r) % COLS) for i in range(blocks)]
        return lax.ppermute(value, "blk", route)

    def ahead(value):
        return lax.ppermute(value, "blk", [(i, (i + COLS) % blocks) for i in range(blocks)])

    row_seg = jnp.stack([segment_ids] + [across(segment_ids, r) for r in (1, 2, 3)])
    slots_here = jnp.broadcast_to(page_table[:, None], (pages, count // pages)).reshape(1, count)
    got = ahead(jnp.concatenate([row_seg, slots_here]))
    prior_seg = jnp.where(index < COLS, -1, got[:COLS])
    slots = got[COLS, :: count // pages] - index * pages
    numbers = jnp.arange(NSEG, dtype=jnp.int32)
    below = jnp.sum(
        (row_seg[None] < numbers[:, None, None]).astype(jnp.int32)
        + (prior_seg[None] < numbers[:, None, None]).astype(jnp.int32),
        axis=(1, 2),
    )
    start = jnp.sum(jnp.where(row_seg[..., None] == numbers, below, 0), axis=-1)
    start_flat = start.reshape(COLS * count)
    start_wide = jnp.broadcast_to(start[..., None], (COLS, count, 128))

    packed = [pack(col, queries, keys, values, half) for half in range(2)]
    row, zrow, zlate, prior = [], [], [], []
    for own, one, two, three, z_now, z_late in packed:
        row.append((own, across(one, 1), across(two, 2), across(three, 3)))
        zrow.append(ahead(z_now))
    for half in range(2):
        passed = ahead(row[half][2][1:])
        prior.append((across(zrow[half][1], 1), passed, across(zrow[half][2], 3)))
    for half in range(2):
        zlate.append(ahead(packed[half][5]))
    pieces = []
    for half in range(2):
        o0, o1, o2, o3 = attend(col, start_flat, start_wide, row[half], zrow[half], prior[half])
        pieces += [o0, across(o1, 1), across(o2, 2), across(o3, 3)]
    mixed = unpack(col, pieces)
    kv = cache(col, slots, zrow[0], zlate[0], zrow[1], zlate[1])
    return (mixed, kv)


def solution(mesh):
    in_specs = (
        P(("req", "blk"), "head"),
        P(("req", "blk"), "head"),
        P(("req", "blk"), "head"),
        P(("req", "blk")),
        P(("req", "blk")),
    )
    out_specs = (P(("req", "blk"), "head"), P(("req", "blk"), None, None, "head"))
    return jax.shard_map(
        per_device, mesh=mesh, in_specs=in_specs, out_specs=out_specs, check_vma=False
    )
```

time: 467 us -> 202 us (0.43)
  the two profiles are of different devices: /device:TPU:16 before, /device:TPU:72 now
where the time goes in v1:
time: 202 us
  waiting for transfers between devices  74 us (37%)
  Pallas kernels  60.8 us (30%)
  starting transfers between devices  53.4 us (26%)
  local copies, waits for them, and re-layouts  12.6 us (6%)
    pallas_call x2, Pallas kernels, attend(): pl.pallas_call(attend_kernel, out_shape=[piece] * 4, in_specs=[SMEM, SMEM...  44.5 us
    ppermute x19, waiting for transfers between devices, across(): return lax.ppermute(value, 'blk', route)  42.5 us
    ppermute x19, starting transfers between devices, across(): return lax.ppermute(value, 'blk', route)  32.5 us
    ppermute x7, waiting for transfers between devices, ahead(): lax.ppermute(value, 'blk', [(i, (i + COLS) % blocks) for i in range(block...  31.5 us
    ppermute x7, starting transfers between devices, ahead(): lax.ppermute(value, 'blk', [(i, (i + COLS) % blocks) for i in range(block...  20.9 us
    unnamed x59, local copies, waits for them, and re-layouts  10.1 us
    pallas_call x2, Pallas kernels, pack(): pl.pallas_call(pack_kernel, grid=(1,), out_shape=[piece] * 4 + [jax.Shape...  8.32 us
    pallas_call x1, Pallas kernels, cache(): pl.pallas_call(cache_kernel, out_shape=jax.ShapeDtypeStruct((COLS, PAGE,...  4.62 us
  transfers between devices with their start and end apart: 26, of which 6 were waited for; matrix products, arithmetic and copies ran while one was open for 1% of the time, Pallas kernels for 26%

profile of v1, /device:TPU:72, one launch (start us, length us, event | category | flops | bytes accessed | tf_op | source)
XLA Modules:
  0.0 202.0 jit_solution(10597765463329503553)
XLA Ops:
  0.6 4.3 %pack.3 = (bf16[3,128,896]{2,1,0:T(8,128)(2,1)S(1)}, bf16[3,128,896]{2,1,0:T(8,128)(2,1)}, bf16[3,128,896]{2,1,0:T(8,128)(2,1)S(1)}, bf16[3,128,896]{2,1,0:T(8,1...) custom-call(s32[1]{0:T(128)} %bitcast.col_ref, bf16[512,1792]{1,0:T(8,128)(2,1)} %q_ref.3, ...), custom_call_target="tpu_custom_call" | custom-call | bytes 6291456 | tf_op jit(solution)/shard_map/pack/pallas_call | solution.py:55
  10.0 4.0 %pack.2 = (bf16[3,128,896]{2,1,0:T(8,128)(2,1)S(1)}, bf16[3,128,896]{2,1,0:T(8,128)(2,1)S(1)}, bf16[3,128,896]{2,1,0:T(8,128)(2,1)S(1)}, bf16[3,128,896]{2,1,0:T...) custom-call(s32[1]{0:T(128)} %bitcast.col_ref, bf16[512,1792]{1,0:T(8,128)(2,1)} %q_ref.3, ...), custom_call_target="tpu_custom_call" | custom-call | bytes 6291456 | tf_op jit(solution)/shard_map/pack/pallas_call | solution.py:55
  18.4 3.1 %collective-permute-start.7 = (bf16[3,2,128,896]{3,2,1,0:T(8,128)(2,1)}, bf16[3,2,128,896]{3,2,1,0:T(8,128)(2,1)S(1)}, u32[]{:S(2)}, u32[]{:S(2)}) collective-permute-start(bf16[3,2,128,896]{3,2,1,0:T(8,128)(2,1)} %get-tuple-element.26), channel_id=1, source_target_pairs={{0,8},{2,10},{4,12},{6,14},{8,16},{10,18},{12,20},{14,22},{16,24},... | collective-permute-start | bytes 4128776 | tf_op jit(solution)/shard_map/ppermute | solution.py:245
  24.8 2.1 %collective-permute-done = s32[512]{0:T(512)S(1)} collective-permute-done((s32[512]{0:T(512)S(1)}, s32[512]{0:T(512)S(1)}, u32[]{:S(2)}, u32[]{:S(2)}) %collective-permute-start) | collective-permute-done | bytes 2080 | tf_op jit(solution)/shard_map/ppermute | solution.py:242
  28.7 3.3 %collective-permute-done.1 = s32[512]{0:T(512)S(1)} collective-permute-done((s32[512]{0:T(512)S(1)}, s32[512]{0:T(512)S(1)}, u32[]{:S(2)}, u32[]{:S(2)}) %collective-permute-start.1) | collective-permute-done | bytes 2080 | tf_op jit(solution)/shard_map/ppermute | solution.py:242
  32.1 3.2 %collective-permute-start.3 = (s32[5,512]{1,0:T(8,128)S(1)}, s32[5,512]{1,0:T(8,128)S(1)}, u32[]{:S(2)}, u32[]{:S(2)}) collective-permute-start(s32[5,512]{1,0:T(8,128)S(1)} %concatenate.4), channel_id=1, source_target_pairs={{0,8},{2,10},{4,12},{6,14},{8,16},{10,18},{12,20},{14,22},{16,24},... | collective-permute-start | bytes 30728 | tf_op jit(solution)/shard_map/ppermute | solution.py:245
  37.1 31.5 %collective-permute-done.3 = s32[5,512]{1,0:T(8,128)S(1)} collective-permute-done((s32[5,512]{1,0:T(8,128)S(1)}, s32[5,512]{1,0:T(8,128)S(1)}, u32[]{:S(2)}, u32[]{:S(2)}) %collective-permute-start.3) | collective-permute-done | bytes 10272 | tf_op jit(solution)/shard_map/ppermute | solution.py:245
  68.6 2.8 %collective-permute-start.16 = (bf16[3,128,896]{2,1,0:T(8,128)(2,1)}, bf16[3,128,896]{2,1,0:T(8,128)(2,1)}, u32[]{:S(2)}, u32[]{:S(2)}) collective-permute-start(bf16[3,128,896]{2,1,0:T(8,128)(2,1)} %copy-done.21), channel_id=1, source_target_pairs={{0,6},{2,0},{4,2},{6,4},{8,14},{10,8},{12,10},{14,12},{16,22},{18,... | collective-permute-start | bytes 2064392 | tf_op jit(solution)/shard_map/ppermute | solution.py:242
  74.0 27.2 %collective-permute-done.16.a3 = bf16[3,128,896]{2,1,0:T(8,128)(2,1)} collective-permute-done((bf16[3,128,896]{2,1,0:T(8,128)(2,1)}, bf16[3,128,896]{2,1,0:T(8,128)(2,1)}, u32[]{:S(2)}, u32[]{:S(2)}) %collective-permute-start.16) | collective-permute-done | bytes 688160 | tf_op jit(solution)/shard_map/ppermute | solution.py:242
  101.2 3.9 %collective-permute-start.6 = (bf16[3,128,896]{2,1,0:T(8,128)(2,1)}, bf16[3,128,896]{2,1,0:T(8,128)(2,1)S(1)}, u32[]{:S(2)}, u32[]{:S(2)}) collective-permute-start(bf16[3,128,896]{2,1,0:T(8,128)(2,1)} %copy-done.18), channel_id=1, source_target_pairs={{0,6},{2,0},{4,2},{6,4},{8,14},{10,8},{12,10},{14,12},{16,22},{18,... | collective-permute-start | bytes 2064392 | tf_op jit(solution)/shard_map/ppermute | solution.py:242
  106.2 2.6 %collective-permute-start.19 = (bf16[2,128,896]{2,1,0:T(8,128)(2,1)S(1)}, bf16[2,128,896]{2,1,0:T(8,128)(2,1)S(1)}, u32[]{:S(2)}, u32[]{:S(2)}) collective-permute-start(bf16[2,128,896]{2,1,0:T(8,128)(2,1)S(1)} %slice.37), channel_id=1, source_target_pairs={{0,8},{2,10},{4,12},{6,14},{8,16},{10,18},{12,20},{14,22},{16,24},... | collective-permute-start | bytes 1376264 | tf_op jit(solution)/shard_map/ppermute | solution.py:245
  109.2 2.0 collective-permute-start.18
  112.3 3.8 %collective-permute-start.9 = (bf16[2,128,896]{2,1,0:T(8,128)(2,1)}, bf16[2,128,896]{2,1,0:T(8,128)(2,1)S(1)}, u32[]{:S(2)}, u32[]{:S(2)}) collective-permute-start(bf16[2,128,896]{2,1,0:T(8,128)(2,1)} %slice.34), channel_id=1, source_target_pairs={{0,8},{2,10},{4,12},{6,14},{8,16},{10,18},{12,20},{14,22},{16,24},... | collective-permute-start | bytes 1376264 | tf_op jit(solution)/shard_map/ppermute | solution.py:245
  116.0 5.2 %collective-permute-done.6.a3 = bf16[3,128,896]{2,1,0:T(8,128)(2,1)S(1)} collective-permute-done((bf16[3,128,896]{2,1,0:T(8,128)(2,1)}, bf16[3,128,896]{2,1,0:T(8,128)(2,1)S(1)}, u32[]{:S(2)}, u32[]{:S(2)}) %collective-permute-start.6) | collective-permute-done | bytes 688160 | tf_op jit(solution)/shard_map/ppermute | solution.py:242
  121.3 3.6 %collective-permute-start.10 = (bf16[2,128,896]{2,1,0:T(8,128)(2,1)S(1)}, bf16[2,128,896]{2,1,0:T(8,128)(2,1)S(1)}, u32[]{:S(2)}, u32[]{:S(2)}) collective-permute-start(bf16[2,128,896]{2,1,0:T(8,128)(2,1)S(1)} %get-tuple-element.44), channel_id=1, source_target_pairs={{0,6},{2,0},{4,2},{6,4},{8,14},{10,8},{12,10},{14,12},{16,22},{18,... | collective-permute-start | bytes 1376264 | tf_op jit(solution)/shard_map/ppermute | solution.py:242
  125.0 4.6 %collective-permute-done.20.p3 = bf16[2,128,896]{2,1,0:T(8,128)(2,1)S(1)} collective-permute-done((bf16[2,128,896]{2,1,0:T(8,128)(2,1)S(1)}, bf16[2,128,896]{2,1,0:T(8,128)(2,1)S(1)}, u32[]{:S(2)}, u32[]{:S(2)}) %collective-permute-start.20) | collective-permute-done | bytes 458784 | tf_op jit(solution)/shard_map/ppermute | solution.py:242
  129.6 2.6 %collective-permute-start.25 = (bf16[2,128,896]{2,1,0:T(8,128)(2,1)S(1)}, bf16[2,128,896]{2,1,0:T(8,128)(2,1)S(1)}, u32[]{:S(2)}, u32[]{:S(2)}) collective-permute-start(bf16[2,128,896]{2,1,0:T(8,128)(2,1)S(1)} %copy-done.24), channel_id=1, source_target_pairs={{0,8},{2,10},{4,12},{6,14},{8,16},{10,18},{12,20},{14,22},{16,24},... | collective-permute-start | bytes 1376264 | tf_op jit(solution)/shard_map/ppermute | solution.py:245
  132.2 3.7 %collective-permute-start.24 = (bf16[2,128,896]{2,1,0:T(8,128)(2,1)S(1)}, bf16[2,128,896]{2,1,0:T(8,128)(2,1)S(1)}, u32[]{:S(2)}, u32[]{:S(2)}) collective-permute-start(bf16[2,128,896]{2,1,0:T(8,128)(2,1)S(1)} %copy-done.26), channel_id=1, source_target_pairs={{0,8},{2,10},{4,12},{6,14},{8,16},{10,18},{12,20},{14,22},{16,24},... | collective-permute-start | bytes 1376264 | tf_op jit(solution)/shard_map/ppermute | solution.py:245
  136.3 22.4 %attend.3 = (bf16[128,896]{1,0:T(8,128)(2,1)S(1)}, bf16[128,896]{1,0:T(8,128)(2,1)S(1)}, bf16[128,896]{1,0:T(8,128)(2,1)}, bf16[128,896]{1,0:T(8,128)(2,1)}) custom-call(s32[1]{0:T(128)} %bitcast.col_ref, s32[2048]{0:T(1024)S(1)} %bitcast.18, s32[4,512,128]{2,1,0:T(8,128)S(1)} %broadcast_in_dim.34.start_ref, bf16[3,128,896]{2,1,0:T(8,128)(2,1)S(1)} %copy-done.15, ...), custom_call_target="tpu_custom_call" | custom-call | flops 4294967296 | bytes 6291456 | tf_op jit(solution)/shard_map/attend/pallas_call | solution.py:162
  158.7 5.1 %collective-permute-start.22 = (bf16[128,896]{1,0:T(8,128)(2,1)}, bf16[128,896]{1,0:T(8,128)(2,1)}, u32[]{:S(2)}, u32[]{:S(2)}) collective-permute-start(bf16[128,896]{1,0:T(8,128)(2,1)} %get-tuple-element.38), channel_id=1, source_target_pairs={{0,4},{2,6},{4,0},{6,2},{8,12},{10,14},{12,8},{14,10},{16,20},{18,... | collective-permute-start | bytes 688136 | tf_op jit(solution)/shard_map/ppermute | solution.py:242
  164.1 22.1 %attend.2 = (bf16[128,896]{1,0:T(8,128)(2,1)S(1)}, bf16[128,896]{1,0:T(8,128)(2,1)}, bf16[128,896]{1,0:T(8,128)(2,1)}, bf16[128,896]{1,0:T(8,128)(2,1)}) custom-call(s32[1]{0:T(128)} %bitcast.col_ref, s32[2048]{0:T(1024)S(1)} %bitcast.19, s32[4,512,128]{2,1,0:T(8,128)S(1)} %broadcast_in_dim.34.start_ref, bf16[3,128,896]{2,1,0:T(8,128)(2,1)S(1)} %copy-done.13, ...), custom_call_target="tpu_custom_call" | custom-call | flops 4294967296 | bytes 6291456 | tf_op jit(solution)/shard_map/attend/pallas_call | solution.py:162
  190.4 2.4 %collective-permute-start.13 = (bf16[128,896]{1,0:T(8,128)(2,1)}, bf16[128,896]{1,0:T(8,128)(2,1)}, u32[]{:S(2)}, u32[]{:S(2)}) collective-permute-start(bf16[128,896]{1,0:T(8,128)(2,1)} %get-tuple-element.30), channel_id=1, source_target_pairs={{0,6},{2,0},{4,2},{6,4},{8,14},{10,8},{12,10},{14,12},{16,22},{18,... | collective-permute-start | bytes 688136 | tf_op jit(solution)/shard_map/ppermute | solution.py:242
  193.9 4.6 %cache.1 = bf16[4,128,2,1792]{3,2,1,0:T(2,128)(2,1)} custom-call(s32[1]{0:T(128)} %bitcast.col_ref, s32[4]{0:T(128)S(1)} %subtract_bitcast_fusion.slot_ref, bf16[3,2,128,896]{3,2,1,0:T(8,128)(2,1)S(1)} %copy-done.3, bf16[2,128,896]{2,1,0:T(8,128)(2,1)S(1)} %copy-done.5, bf16[3,2,128,896]{3,2,1,0:T(8,128)(2,1)S(1)} %copy-done.1, ...), custom_call_target="tpu_custom_call" | custom-call | bytes 8388608 | tf_op jit(solution)/shard_map/cache/pallas_call | solution.py:221
  198.6 3.4 %unpack.1 = bf16[512,1792]{1,0:T(8,128)(2,1)} custom-call(s32[1]{0:T(128)} %bitcast.col_ref, bf16[128,896]{1,0:T(8,128)(2,1)S(1)} %copy-done.11, bf16[128,896]{1,0:T(8,128)(2,1)} %collective-permute-done.11.refs_1_, bf16[128,896]{1,0:T(8,128)(2,1)} %collective-permute-done.12.refs_2_, bf16[128,896]{1,0:T(8,128)(2,1)} %collective-permute-done.13.refs_3_, ...), custom_call_target="tpu_custom_call" | custom-call | bytes 4194304 | tf_op jit(solution)/shard_map/unpack/pallas_call | solution.py:195
  (106 shorter events, 27.6 us)
Async XLA Ops:
  6.6 99.5 %collective-permute-start.17 = (bf16[3,2,128,896]{3,2,1,0:T(8,128)(2,1)}, bf16[3,2,128,896]{3,2,1,0:T(8,128)(2,1)S(1)}, u32[]{:S(2)}, u32[]{:S(2)}) collective-permute-start(bf16[3,2,128,896]{3,2,1,0:T(8,128)(2,1)} %get-tuple-element.35), channel_id=1, source_target_pairs={{0,8},{2,10},{4,12},{6,14},{8,16},{10,18},{12,20},{14,22},{16,24},... | collective-permute-start | bytes 4128776 | tf_op jit(solution)/shard_map/ppermute | solution.py:245
  8.5 62.8 %collective-permute-start.14 = (bf16[3,128,896]{2,1,0:T(8,128)(2,1)}, bf16[3,128,896]{2,1,0:T(8,128)(2,1)S(1)}, u32[]{:S(2)}, u32[]{:S(2)}) collective-permute-start(bf16[3,128,896]{2,1,0:T(8,128)(2,1)} %get-tuple-element.32), channel_id=1, source_target_pairs={{0,2},{2,4},{4,6},{6,0},{8,10},{10,12},{12,14},{14,8},{16,18},{18,... | collective-permute-start | bytes 2064392 | tf_op jit(solution)/shard_map/ppermute | solution.py:242
  18.4 90.8 %collective-permute-start.7 = (bf16[3,2,128,896]{3,2,1,0:T(8,128)(2,1)}, bf16[3,2,128,896]{3,2,1,0:T(8,128)(2,1)S(1)}, u32[]{:S(2)}, u32[]{:S(2)}) collective-permute-start(bf16[3,2,128,896]{3,2,1,0:T(8,128)(2,1)} %get-tuple-element.26), channel_id=1, source_target_pairs={{0,8},{2,10},{4,12},{6,14},{8,16},{10,18},{12,20},{14,22},{16,24},... | collective-permute-start | bytes 4128776 | tf_op jit(solution)/shard_map/ppermute | solution.py:245
  23.0 5.7 %collective-permute-start.2 = (s32[512]{0:T(512)S(1)}, s32[512]{0:T(512)S(1)}, u32[]{:S(2)}, u32[]{:S(2)}) collective-permute-start(s32[512]{0:T(512)S(1)} %copy-done.27), channel_id=1, source_target_pairs={{0,6},{2,0},{4,2},{6,4},{8,14},{10,8},{12,10},{14,12},{16,22},{18,... | collective-permute-start | bytes 6152 | tf_op jit(solution)/shard_map/ppermute | solution.py:242
  32.1 36.5 %collective-permute-start.3 = (s32[5,512]{1,0:T(8,128)S(1)}, s32[5,512]{1,0:T(8,128)S(1)}, u32[]{:S(2)}, u32[]{:S(2)}) collective-permute-start(s32[5,512]{1,0:T(8,128)S(1)} %concatenate.4), channel_id=1, source_target_pairs={{0,8},{2,10},{4,12},{6,14},{8,16},{10,18},{12,20},{14,22},{16,24},... | collective-permute-start | bytes 30728 | tf_op jit(solution)/shard_map/ppermute | solution.py:245
  35.3 37.7 %collective-permute-start.15 = (bf16[3,128,896]{2,1,0:T(8,128)(2,1)}, bf16[3,128,896]{2,1,0:T(8,128)(2,1)}, u32[]{:S(2)}, u32[]{:S(2)}) collective-permute-start(bf16[3,128,896]{2,1,0:T(8,128)(2,1)} %copy-done.22), channel_id=1, source_target_pairs={{0,4},{2,6},{4,0},{6,2},{8,12},{10,14},{12,8},{14,10},{16,20},{18,... | collective-permute-start | bytes 2064392 | tf_op jit(solution)/shard_map/ppermute | solution.py:242
  68.6 32.6 %collective-permute-start.16 = (bf16[3,128,896]{2,1,0:T(8,128)(2,1)}, bf16[3,128,896]{2,1,0:T(8,128)(2,1)}, u32[]{:S(2)}, u32[]{:S(2)}) collective-permute-start(bf16[3,128,896]{2,1,0:T(8,128)(2,1)} %copy-done.21), channel_id=1, source_target_pairs={{0,6},{2,0},{4,2},{6,4},{8,14},{10,8},{12,10},{14,12},{16,22},{18,... | collective-permute-start | bytes 2064392 | tf_op jit(solution)/shard_map/ppermute | solution.py:242
  72.2 36.7 %collective-permute-start.5 = (bf16[3,128,896]{2,1,0:T(8,128)(2,1)}, bf16[3,128,896]{2,1,0:T(8,128)(2,1)S(1)}, u32[]{:S(2)}, u32[]{:S(2)}) collective-permute-start(bf16[3,128,896]{2,1,0:T(8,128)(2,1)} %copy-done.20), channel_id=1, source_target_pairs={{0,4},{2,6},{4,0},{6,2},{8,12},{10,14},{12,8},{14,10},{16,20},{18,... | collective-permute-start | bytes 2064392 | tf_op jit(solution)/shard_map/ppermute | solution.py:242
  73.0 39.2 %collective-permute-start.4 = (bf16[3,128,896]{2,1,0:T(8,128)(2,1)}, bf16[3,128,896]{2,1,0:T(8,128)(2,1)S(1)}, u32[]{:S(2)}, u32[]{:S(2)}) collective-permute-start(bf16[3,128,896]{2,1,0:T(8,128)(2,1)} %copy-done.19), channel_id=1, source_target_pairs={{0,2},{2,4},{4,6},{6,0},{8,10},{10,12},{12,14},{14,8},{16,18},{18,... | collective-permute-start | bytes 2064392 | tf_op jit(solution)/shard_map/ppermute | solution.py:242
  101.2 20.1 %collective-permute-start.6 = (bf16[3,128,896]{2,1,0:T(8,128)(2,1)}, bf16[3,128,896]{2,1,0:T(8,128)(2,1)S(1)}, u32[]{:S(2)}, u32[]{:S(2)}) collective-permute-start(bf16[3,128,896]{2,1,0:T(8,128)(2,1)} %copy-done.18), channel_id=1, source_target_pairs={{0,6},{2,0},{4,2},{6,4},{8,14},{10,8},{12,10},{14,12},{16,22},{18,... | collective-permute-start | bytes 2064392 | tf_op jit(solution)/shard_map/ppermute | solution.py:242
  106.2 18.7 %collective-permute-start.19 = (bf16[2,128,896]{2,1,0:T(8,128)(2,1)S(1)}, bf16[2,128,896]{2,1,0:T(8,128)(2,1)S(1)}, u32[]{:S(2)}, u32[]{:S(2)}) collective-permute-start(bf16[2,128,896]{2,1,0:T(8,128)(2,1)S(1)} %slice.37), channel_id=1, source_target_pairs={{0,8},{2,10},{4,12},{6,14},{8,16},{10,18},{12,20},{14,22},{16,24},... | collective-permute-start | bytes 1376264 | tf_op jit(solution)/shard_map/ppermute | solution.py:245
  108.9 20.7 %collective-permute-start.20 = (bf16[2,128,896]{2,1,0:T(8,128)(2,1)S(1)}, bf16[2,128,896]{2,1,0:T(8,128)(2,1)S(1)}, u32[]{:S(2)}, u32[]{:S(2)}) collective-permute-start(bf16[2,128,896]{2,1,0:T(8,128)(2,1)S(1)} %get-tuple-element.42), channel_id=1, source_target_pairs={{0,6},{2,0},{4,2},{6,4},{8,14},{10,8},{12,10},{14,12},{16,22},{18,... | collective-permute-start | bytes 1376264 | tf_op jit(solution)/shard_map/ppermute | solution.py:242
  109.2 23.0 %collective-permute-start.18 = (bf16[2,128,896]{2,1,0:T(8,128)(2,1)S(1)}, bf16[2,128,896]{2,1,0:T(8,128)(2,1)S(1)}, u32[]{:S(2)}, u32[]{:S(2)}) collective-permute-start(bf16[2,128,896]{2,1,0:T(8,128)(2,1)S(1)} %get-tuple-element.43), channel_id=1, source_target_pairs={{0,2},{2,4},{4,6},{6,0},{8,10},{10,12},{12,14},{14,8},{16,18},{18,... | collective-permute-start | bytes 1376264 | tf_op jit(solution)/shard_map/ppermute | solution.py:242
  112.3 46.4 %collective-permute-start.9 = (bf16[2,128,896]{2,1,0:T(8,128)(2,1)}, bf16[2,128,896]{2,1,0:T(8,128)(2,1)S(1)}, u32[]{:S(2)}, u32[]{:S(2)}) collective-permute-start(bf16[2,128,896]{2,1,0:T(8,128)(2,1)} %slice.34), channel_id=1, source_target_pairs={{0,8},{2,10},{4,12},{6,14},{8,16},{10,18},{12,20},{14,22},{16,24},... | collective-permute-start | bytes 1376264 | tf_op jit(solution)/shard_map/ppermute | solution.py:245
  121.3 37.4 %collective-permute-start.10 = (bf16[2,128,896]{2,1,0:T(8,128)(2,1)S(1)}, bf16[2,128,896]{2,1,0:T(8,128)(2,1)S(1)}, u32[]{:S(2)}, u32[]{:S(2)}) collective-permute-start(bf16[2,128,896]{2,1,0:T(8,128)(2,1)S(1)} %get-tuple-element.44), channel_id=1, source_target_pairs={{0,6},{2,0},{4,2},{6,4},{8,14},{10,8},{12,10},{14,12},{16,22},{18,... | collective-permute-start | bytes 1376264 | tf_op jit(solution)/shard_map/ppermute | solution.py:242
  124.9 39.0 %collective-permute-start.8 = (bf16[2,128,896]{2,1,0:T(8,128)(2,1)S(1)}, bf16[2,128,896]{2,1,0:T(8,128)(2,1)S(1)}, u32[]{:S(2)}, u32[]{:S(2)}) collective-permute-start(bf16[2,128,896]{2,1,0:T(8,128)(2,1)S(1)} %get-tuple-element.45), channel_id=1, source_target_pairs={{0,2},{2,4},{4,6},{6,0},{8,10},{10,12},{12,14},{14,8},{16,18},{18,... | collective-permute-start | bytes 1376264 | tf_op jit(solution)/shard_map/ppermute | solution.py:242
  129.6 57.2 %collective-permute-start.25 = (bf16[2,128,896]{2,1,0:T(8,128)(2,1)S(1)}, bf16[2,128,896]{2,1,0:T(8,128)(2,1)S(1)}, u32[]{:S(2)}, u32[]{:S(2)}) collective-permute-start(bf16[2,128,896]{2,1,0:T(8,128)(2,1)S(1)} %copy-done.24), channel_id=1, source_target_pairs={{0,8},{2,10},{4,12},{6,14},{8,16},{10,18},{12,20},{14,22},{16,24},... | collective-permute-start | bytes 1376264 | tf_op jit(solution)/shard_map/ppermute | solution.py:245
  132.2 56.4 %collective-permute-start.24 = (bf16[2,128,896]{2,1,0:T(8,128)(2,1)S(1)}, bf16[2,128,896]{2,1,0:T(8,128)(2,1)S(1)}, u32[]{:S(2)}, u32[]{:S(2)}) collective-permute-start(bf16[2,128,896]{2,1,0:T(8,128)(2,1)S(1)} %copy-done.26), channel_id=1, source_target_pairs={{0,8},{2,10},{4,12},{6,14},{8,16},{10,18},{12,20},{14,22},{16,24},... | collective-permute-start | bytes 1376264 | tf_op jit(solution)/shard_map/ppermute | solution.py:245
  158.7 31.1 %collective-permute-start.21 = (bf16[128,896]{1,0:T(8,128)(2,1)S(1)}, bf16[128,896]{1,0:T(8,128)(2,1)S(1)}, u32[]{:S(2)}, u32[]{:S(2)}) collective-permute-start(bf16[128,896]{1,0:T(8,128)(2,1)S(1)} %get-tuple-element.37), channel_id=1, source_target_pairs={{0,2},{2,4},{4,6},{6,0},{8,10},{10,12},{12,14},{14,8},{16,18},{18,... | collective-permute-start | bytes 688136 | tf_op jit(solution)/shard_map/ppermute | solution.py:242
  158.7 39.9 %collective-permute-start.22 = (bf16[128,896]{1,0:T(8,128)(2,1)}, bf16[128,896]{1,0:T(8,128)(2,1)}, u32[]{:S(2)}, u32[]{:S(2)}) collective-permute-start(bf16[128,896]{1,0:T(8,128)(2,1)} %get-tuple-element.38), channel_id=1, source_target_pairs={{0,4},{2,6},{4,0},{6,2},{8,12},{10,14},{12,8},{14,10},{16,20},{18,... | collective-permute-start | bytes 688136 | tf_op jit(solution)/shard_map/ppermute | solution.py:242
  163.8 34.7 %collective-permute-start.23 = (bf16[128,896]{1,0:T(8,128)(2,1)}, bf16[128,896]{1,0:T(8,128)(2,1)}, u32[]{:S(2)}, u32[]{:S(2)}) collective-permute-start(bf16[128,896]{1,0:T(8,128)(2,1)} %get-tuple-element.39), channel_id=1, source_target_pairs={{0,6},{2,0},{4,2},{6,4},{8,14},{10,8},{12,10},{14,12},{16,22},{18,... | collective-permute-start | bytes 688136 | tf_op jit(solution)/shard_map/ppermute | solution.py:242
  186.9 11.7 %collective-permute-start.11 = (bf16[128,896]{1,0:T(8,128)(2,1)}, bf16[128,896]{1,0:T(8,128)(2,1)}, u32[]{:S(2)}, u32[]{:S(2)}) collective-permute-start(bf16[128,896]{1,0:T(8,128)(2,1)} %get-tuple-element.28), channel_id=1, source_target_pairs={{0,2},{2,4},{4,6},{6,0},{8,10},{10,12},{12,14},{14,8},{16,18},{18,... | collective-permute-start | bytes 688136 | tf_op jit(solution)/shard_map/ppermute | solution.py:242
  189.4 9.1 %collective-permute-start.12 = (bf16[128,896]{1,0:T(8,128)(2,1)}, bf16[128,896]{1,0:T(8,128)(2,1)}, u32[]{:S(2)}, u32[]{:S(2)}) collective-permute-start(bf16[128,896]{1,0:T(8,128)(2,1)} %get-tuple-element.29), channel_id=1, source_target_pairs={{0,4},{2,6},{4,0},{6,2},{8,12},{10,14},{12,8},{14,10},{16,20},{18,... | collective-permute-start | bytes 688136 | tf_op jit(solution)/shard_map/ppermute | solution.py:242
  190.4 8.1 %collective-permute-start.13 = (bf16[128,896]{1,0:T(8,128)(2,1)}, bf16[128,896]{1,0:T(8,128)(2,1)}, u32[]{:S(2)}, u32[]{:S(2)}) collective-permute-start(bf16[128,896]{1,0:T(8,128)(2,1)} %get-tuple-element.30), channel_id=1, source_target_pairs={{0,6},{2,0},{4,2},{6,4},{8,14},{10,8},{12,10},{14,12},{16,22},{18,... | collective-permute-start | bytes 688136 | tf_op jit(solution)/shard_map/ppermute | solution.py:242
  (31 other events, 294.2 us)

commit v2 on v1

--- a/solution.py
+++ b/solution.py
@@ -31,7 +31,8 @@
     ]
 
 
-def pack_kernel(col_ref, q_ref, k_ref, v_ref, own, one, two, three, zrow, zlate, held):
+def pack_kernel(col_ref, q_ref, k_ref, v_ref, *refs):
+    own, one, two, three, zrow, zlate, held = refs[-7:]
     col = col_ref[0]
     outs = (own, one, two, three)
     for t, ref in enumerate((q_ref, k_ref, v_ref)):
@@ -49,7 +50,7 @@
                 zrow[(0, 1, None, 2)[r], t] = held[t + 1, slot]
 
 
-def pack(col, queries, keys, values, half):
+def pack(col, queries, keys, values, half, after):
     block = pl.BlockSpec((COLS * PAGE, SLAB), lambda i: (0, half))
     piece = jax.ShapeDtypeStruct((3, PAGE, SLAB), jnp.bfloat16)
     return pl.pallas_call(
@@ -60,13 +61,13 @@
             jax.ShapeDtypeStruct((3, 2, PAGE, SLAB), jnp.bfloat16),
             jax.ShapeDtypeStruct((2, PAGE, SLAB), jnp.bfloat16),
         ],
-        in_specs=[SMEM, block, block, block],
+        in_specs=[SMEM, block, block, block] + [pl.BlockSpec(memory_space=pl.ANY)] * len(after),
         out_specs=[VMEM] * 6,
         scratch_shapes=[pltpu.VMEM((3, COLS, PAGE, SLAB), jnp.bfloat16)],
         compiler_params=params(),
         name="pack",
         cost_estimate=pl.CostEstimate(flops=0, transcendentals=0, bytes_accessed=6 * 1024 * 1024),
-    )(col, queries, keys, values)
+    )(col, queries, keys, values, *after)
 
 
 def attend_kernel(
@@ -244,37 +245,46 @@
     def ahead(value):
         return lax.ppermute(value, "blk", [(i, (i + COLS) % blocks) for i in range(blocks)])
 
-    row_seg = jnp.stack([segment_ids] + [across(segment_ids, r) for r in (1, 2, 3)])
-    slots_here = jnp.broadcast_to(page_table[:, None], (pages, count // pages)).reshape(1, count)
-    got = ahead(jnp.concatenate([row_seg, slots_here]))
-    prior_seg = jnp.where(index < COLS, -1, got[:COLS])
-    slots = got[COLS, :: count // pages] - index * pages
+    def behind(value, *done):
+        return lax.optimization_barrier((value, *done))[0]
+
     numbers = jnp.arange(NSEG, dtype=jnp.int32)
-    below = jnp.sum(
-        (row_seg[None] < numbers[:, None, None]).astype(jnp.int32)
-        + (prior_seg[None] < numbers[:, None, None]).astype(jnp.int32),
-        axis=(1, 2),
+    below = jnp.sum((segment_ids < numbers[:, None]).astype(jnp.int32), axis=1)
+    named = lax.dynamic_update_slice(
+        jnp.zeros((blocks * pages,), jnp.int32), page_table, (index * pages,)
     )
-    start = jnp.sum(jnp.where(row_seg[..., None] == numbers, below, 0), axis=-1)
-    start_flat = start.reshape(COLS * count)
+    shared = lax.psum(jnp.concatenate([below, named]), "blk")
+    source = lax.rem(index + blocks - COLS, blocks)
+    slots = lax.dynamic_slice(shared, (NSEG + source * pages,), (pages,)) - index * pages
+    width = COLS * count
+    at = COLS * count - lax.div(index, COLS) * width
+    home = jnp.stack([lax.rem(col[0] - r + COLS, COLS) for r in range(COLS)])
+    here = width + home[:, None] * count + jnp.arange(count, dtype=jnp.int32)
+    begin = shared[:NSEG] + at
+    start = jnp.max(
+        jnp.where(begin <= here[..., None], begin, -(2**30)), axis=-1
+    ).astype(jnp.int32)
+    start_flat = start.reshape(width)
     start_wide = jnp.broadcast_to(start[..., None], (COLS, count, 128))
 
-    packed = [pack(col, queries, keys, values, half) for half in range(2)]
-    row, zrow, zlate, prior = [], [], [], []
-    for own, one, two, three, z_now, z_late in packed:
-        row.append((own, across(one, 1), across(two, 2), across(three, 3)))
-        zrow.append(ahead(z_now))
+    pieces, late, zrows, wait, attended = [], [], [], (), None
     for half in range(2):
-        passed = ahead(row[half][2][1:])
-        prior.append((across(zrow[half][1], 1), passed, across(zrow[half][2], 3)))
-    for half in range(2):
-        zlate.append(ahead(packed[half][5]))
-    pieces = []
-    for half in range(2):
-        o0, o1, o2, o3 = attend(col, start_flat, start_wide, row[half], zrow[half], prior[half])
-        pieces += [o0, across(o1, 1), across(o2, 2), across(o3, 3)]
+        own, one, two, three, z_now, z_late = pack(col, queries, keys, values, half, wait)
+        zrow = ahead(z_now)
+        row = (own, across(one, 1), across(two, 2), across(three, 3))
+        wait = (zrow, row[2])
+        from_z1, from_row, from_z3 = zrow[1], row[2][1:], zrow[2]
+        if attended is not None:
+            from_z1, from_row, from_z3 = (behind(x, attended) for x in (from_z1, from_row, from_z3))
+        prior = (across(from_z1, 1), ahead(from_row), across(from_z3, 3))
+        outs = attend(col, start_flat, start_wide, row, zrow, prior)
+        attended = outs[0]
+        pieces += [outs[0]] + [across(outs[r], r) for r in (1, 2, 3)]
+        late.append(z_late)
+        zrows.append(zrow)
+    late = [ahead(behind(x, zrows[1])) for x in late]
     mixed = unpack(col, pieces)
-    kv = cache(col, slots, zrow[0], zlate[0], zrow[1], zlate[1])
+    kv = cache(col, slots, zrows[0], late[0], zrows[1], late[1])
     return (mixed, kv)
 
 

time: 202 us -> 196 us (0.970)
  the two profiles are of different devices: /device:TPU:72 before, /device:TPU:16 now
where the time goes in v2:
time: 196 us; the launch traced here: 193 us
  waiting for transfers between devices  51.6 us (26%)
  Pallas kernels  50.7 us (26%)
  starting transfers between devices  42.7 us (22%)
  blocking collectives  34.1 us (17%)
  local copies, waits for them, and re-layouts  12.7 us (6%)
    pallas_call x2, Pallas kernels, attend(): pl.pallas_call(attend_kernel, out_shape=[piece] * 4, in_specs=[SMEM, SMEM...  34.6 us
    psum x1, blocking collectives, per_device(): shared = lax.psum(jnp.concatenate([below, named]), 'blk')  34.1 us
    ppermute x16, waiting for transfers between devices, across(): return lax.ppermute(value, 'blk', route)  33.1 us
    ppermute x16, starting transfers between devices, across(): return lax.ppermute(value, 'blk', route)  29 us
    ppermute x6, waiting for transfers between devices, ahead(): lax.ppermute(value, 'blk', [(i, (i + COLS) % blocks) for i in range(block...  18.5 us
    ppermute x6, starting transfers between devices, ahead(): lax.ppermute(value, 'blk', [(i, (i + COLS) % blocks) for i in range(block...  13.7 us
    unnamed x53, local copies, waits for them, and re-layouts  10.8 us
    pallas_call x2, Pallas kernels, pack(): pl.pallas_call(pack_kernel, grid=(1,), out_shape=[piece] * 4 + [jax.Shape...  8.28 us
  transfers between devices with their start and end apart: 22, of which 6 were waited for; matrix products, arithmetic and copies ran while one was open for 1% of the time, Pallas kernels for 22%

profile of v2, /device:TPU:16, one launch (start us, length us, event | category | flops | bytes accessed | tf_op | source)
XLA Modules:
  0.0 193.1 jit_solution(16391200229773142073)
XLA Ops:
  0.7 4.3 %pack.2 = (bf16[3,128,896]{2,1,0:T(8,128)(2,1)S(1)}, bf16[3,128,896]{2,1,0:T(8,128)(2,1)}, bf16[3,128,896]{2,1,0:T(8,128)(2,1)}, bf16[3,128,896]{2,1,0:T(8,128)(...) custom-call(s32[1]{0:T(128)} %bitcast.col_ref, bf16[512,1792]{1,0:T(8,128)(2,1)} %q_ref.3, ...), custom_call_target="tpu_custom_call" | custom-call | bytes 6291456 | tf_op jit(solution)/shard_map/pack/pallas_call | solution.py:56
  8.5 3.0 %collective-permute-start.1 = (bf16[3,128,896]{2,1,0:T(8,128)(2,1)}, bf16[3,128,896]{2,1,0:T(8,128)(2,1)S(1)}, u32[]{:S(2)}, u32[]{:S(2)}) collective-permute-start(bf16[3,128,896]{2,1,0:T(8,128)(2,1)} %get-tuple-element.29), channel_id=1, source_target_pairs={{0,4},{2,6},{4,0},{6,2},{8,12},{10,14},{12,8},{14,10},{16,20},{18,... | collective-permute-start | bytes 2064392 | tf_op jit(solution)/shard_map/ppermute | solution.py:243
  12.1 2.6 %collective-permute-start.2 = (bf16[3,128,896]{2,1,0:T(8,128)(2,1)}, bf16[3,128,896]{2,1,0:T(8,128)(2,1)}, u32[]{:S(2)}, u32[]{:S(2)}) collective-permute-start(bf16[3,128,896]{2,1,0:T(8,128)(2,1)} %get-tuple-element.30), channel_id=1, source_target_pairs={{0,6},{2,0},{4,2},{6,4},{8,14},{10,8},{12,10},{14,12},{16,22},{18,... | collective-permute-start | bytes 2064392 | tf_op jit(solution)/shard_map/ppermute | solution.py:243
  15.1 13.5 %collective-permute-done.1.a2.refs_1_ = bf16[3,128,896]{2,1,0:T(8,128)(2,1)S(1)} collective-permute-done((bf16[3,128,896]{2,1,0:T(8,128)(2,1)}, bf16[3,128,896]{2,1,0:T(8,128)(2,1)S(1)}, u32[]{:S(2)}, u32[]{:S(2)}) %collective-permute-start.1) | collective-permute-done | bytes 688160 | tf_op jit(solution)/shard_map/ppermute | solution.py:243
  28.6 14.0 %collective-permute-done.3.zrow.refs_0_.zrow_a = bf16[3,2,128,896]{3,2,1,0:T(8,128)(2,1)S(1)} collective-permute-done((bf16[3,2,128,896]{3,2,1,0:T(8,128)(2,1)S(1)}, bf16[3,2,128,896]{3,2,1,0:T(8,128)(2,1)S(1)}, u32[]{:S(2)}, u32[]{:S(2)}) %collective-permute-start.3) | collective-permute-done | bytes 1376288 | tf_op jit(solution)/shard_map/ppermute | solution.py:246
  43.7 4.0 %pack.3 = (bf16[3,128,896]{2,1,0:T(8,128)(2,1)S(1)}, bf16[3,128,896]{2,1,0:T(8,128)(2,1)S(1)}, bf16[3,128,896]{2,1,0:T(8,128)(2,1)S(1)}, bf16[3,128,896]{2,1,0:T...) custom-call(s32[1]{0:T(128)} %bitcast.col_ref, bf16[512,1792]{1,0:T(8,128)(2,1)} %q_ref.3, ...), custom_call_target="tpu_custom_call" | custom-call | bytes 6291456 | tf_op jit(solution)/shard_map/pack/pallas_call | solution.py:56
  52.0 34.1 %psum.7 = s32[144]{0:T(256)S(1)} all-reduce(s32[144]{0:T(256)S(1)} %pad_add_fusion), channel_id=1, replica_groups=mesh['req'=4,'blk'=32,'head'=2] {'blk'}, use_global_device_ids=true, to_apply=%region_1.0 | all-reduce | flops 144 | bytes 1152 | tf_op jit(solution)/shard_map/psum | solution.py:256
  86.2 6.2 %collective-permute-start.5 = (bf16[2,128,896]{2,1,0:T(8,128)(2,1)S(1)}, bf16[2,128,896]{2,1,0:T(8,128)(2,1)S(1)}, u32[]{:S(2)}, u32[]{:S(2)}) collective-permute-start(bf16[2,128,896]{2,1,0:T(8,128)(2,1)S(1)} %slice.29), channel_id=1, source_target_pairs={{0,8},{2,10},{4,12},{6,14},{8,16},{10,18},{12,20},{14,22},{16,24},... | collective-permute-start | bytes 1376264 | tf_op jit(solution)/shard_map/ppermute | solution.py:246
  93.6 2.8 %collective-permute-start.6 = (bf16[2,128,896]{2,1,0:T(8,128)(2,1)S(1)}, bf16[2,128,896]{2,1,0:T(8,128)(2,1)S(1)}, u32[]{:S(2)}, u32[]{:S(2)}) collective-permute-start(bf16[2,128,896]{2,1,0:T(8,128)(2,1)S(1)} %get-tuple-element.54), channel_id=1, source_target_pairs={{0,6},{2,0},{4,2},{6,4},{8,14},{10,8},{12,10},{14,12},{16,22},{18,... | collective-permute-start | bytes 1376264 | tf_op jit(solution)/shard_map/ppermute | solution.py:243
  96.5 2.3 %collective-permute-start.11 = (bf16[3,128,896]{2,1,0:T(8,128)(2,1)S(1)}, bf16[3,128,896]{2,1,0:T(8,128)(2,1)S(1)}, u32[]{:S(2)}, u32[]{:S(2)}) collective-permute-start(bf16[3,128,896]{2,1,0:T(8,128)(2,1)S(1)} %copy-done.19), channel_id=1, source_target_pairs={{0,4},{2,6},{4,0},{6,2},{8,12},{10,14},{12,8},{14,10},{16,20},{18,... | collective-permute-start | bytes 2064392 | tf_op jit(solution)/shard_map/ppermute | solution.py:243
  101.4 16.2 %collective-permute-done.6.p3 = bf16[2,128,896]{2,1,0:T(8,128)(2,1)S(1)} collective-permute-done((bf16[2,128,896]{2,1,0:T(8,128)(2,1)S(1)}, bf16[2,128,896]{2,1,0:T(8,128)(2,1)S(1)}, u32[]{:S(2)}, u32[]{:S(2)}) %collective-permute-start.6) | collective-permute-done | bytes 458784 | tf_op jit(solution)/shard_map/ppermute | solution.py:243
  117.6 4.2 %collective-permute-start.12 = (bf16[3,128,896]{2,1,0:T(8,128)(2,1)S(1)}, bf16[3,128,896]{2,1,0:T(8,128)(2,1)S(1)}, u32[]{:S(2)}, u32[]{:S(2)}) collective-permute-start(bf16[3,128,896]{2,1,0:T(8,128)(2,1)S(1)} %copy-done.15), channel_id=1, source_target_pairs={{0,6},{2,0},{4,2},{6,4},{8,14},{10,8},{12,10},{14,12},{16,22},{18,... | collective-permute-start | bytes 2064392 | tf_op jit(solution)/shard_map/ppermute | solution.py:243
  121.8 3.3 %collective-permute-done.4.p1 = bf16[2,128,896]{2,1,0:T(8,128)(2,1)S(1)} collective-permute-done((bf16[2,128,896]{2,1,0:T(8,128)(2,1)S(1)}, bf16[2,128,896]{2,1,0:T(8,128)(2,1)S(1)}, u32[]{:S(2)}, u32[]{:S(2)}) %collective-permute-start.4) | collective-permute-done | bytes 458784 | tf_op jit(solution)/shard_map/ppermute | solution.py:243
  125.5 17.4 %attend.2 = (bf16[128,896]{1,0:T(8,128)(2,1)S(1)}, bf16[128,896]{1,0:T(8,128)(2,1)S(1)}, bf16[128,896]{1,0:T(8,128)(2,1)}, bf16[128,896]{1,0:T(8,128)(2,1)}) custom-call(s32[1]{0:T(128)} %bitcast.col_ref, s32[2048]{0:T(1024)S(1)} %bitcast.15, s32[4,512,128]{2,1,0:T(8,128)S(1)} %broadcast_in_dim.12.start_ref, bf16[3,128,896]{2,1,0:T(8,128)(2,1)S(1)} %copy-done.13, ...), custom_call_target="tpu_custom_call" | custom-call | flops 4294967296 | bytes 6291456 | tf_op jit(solution)/shard_map/attend/pallas_call | solution.py:163
  143.7 3.2 %collective-permute-start.16 = (bf16[2,128,896]{2,1,0:T(8,128)(2,1)S(1)}, bf16[2,128,896]{2,1,0:T(8,128)(2,1)S(1)}, u32[]{:S(2)}, u32[]{:S(2)}) collective-permute-start(bf16[2,128,896]{2,1,0:T(8,128)(2,1)S(1)} %get-tuple-element.43), channel_id=1, source_target_pairs={{0,6},{2,0},{4,2},{6,4},{8,14},{10,8},{12,10},{14,12},{16,22},{18,... | collective-permute-start | bytes 1376264 | tf_op jit(solution)/shard_map/ppermute | solution.py:243
  146.9 2.8 %collective-permute-start.20 = (bf16[2,128,896]{2,1,0:T(8,128)(2,1)S(1)}, bf16[2,128,896]{2,1,0:T(8,128)(2,1)S(1)}, u32[]{:S(2)}, u32[]{:S(2)}) collective-permute-start(bf16[2,128,896]{2,1,0:T(8,128)(2,1)S(1)} %copy-done.21), channel_id=1, source_target_pairs={{0,8},{2,10},{4,12},{6,14},{8,16},{10,18},{12,20},{14,22},{16,24},... | collective-permute-start | bytes 1376264 | tf_op jit(solution)/shard_map/ppermute | solution.py:246
  149.7 2.3 %collective-permute-start.21 = (bf16[2,128,896]{2,1,0:T(8,128)(2,1)S(1)}, bf16[2,128,896]{2,1,0:T(8,128)(2,1)S(1)}, u32[]{:S(2)}, u32[]{:S(2)}) collective-permute-start(bf16[2,128,896]{2,1,0:T(8,128)(2,1)S(1)} %copy-done.23), channel_id=1, source_target_pairs={{0,8},{2,10},{4,12},{6,14},{8,16},{10,18},{12,20},{14,22},{16,24},... | collective-permute-start | bytes 1376264 | tf_op jit(solution)/shard_map/ppermute | solution.py:246
  152.0 3.4 %collective-permute-done.15.p2 = bf16[2,128,896]{2,1,0:T(8,128)(2,1)S(1)} collective-permute-done((bf16[2,128,896]{2,1,0:T(8,128)(2,1)S(1)}, bf16[2,128,896]{2,1,0:T(8,128)(2,1)S(1)}, u32[]{:S(2)}, u32[]{:S(2)}) %collective-permute-start.15) | collective-permute-done | bytes 458784 | tf_op jit(solution)/shard_map/ppermute | solution.py:246
  156.2 2.4 %collective-permute-start.9 = (bf16[128,896]{1,0:T(8,128)(2,1)}, bf16[128,896]{1,0:T(8,128)(2,1)}, u32[]{:S(2)}, u32[]{:S(2)}) collective-permute-start(bf16[128,896]{1,0:T(8,128)(2,1)} %get-tuple-element.35), channel_id=1, source_target_pairs={{0,6},{2,0},{4,2},{6,4},{8,14},{10,8},{12,10},{14,12},{16,22},{18,... | collective-permute-start | bytes 688136 | tf_op jit(solution)/shard_map/ppermute | solution.py:243
  158.7 17.2 %attend.3 = (bf16[128,896]{1,0:T(8,128)(2,1)S(1)}, bf16[128,896]{1,0:T(8,128)(2,1)}, bf16[128,896]{1,0:T(8,128)(2,1)}, bf16[128,896]{1,0:T(8,128)(2,1)}) custom-call(s32[1]{0:T(128)} %bitcast.col_ref, s32[2048]{0:T(1024)S(1)} %bitcast.16, s32[4,512,128]{2,1,0:T(8,128)S(1)} %broadcast_in_dim.12.start_ref, bf16[3,128,896]{2,1,0:T(8,128)(2,1)S(1)} %copy-done.11, ...), custom_call_target="tpu_custom_call" | custom-call | flops 4294967296 | bytes 6291456 | tf_op jit(solution)/shard_map/attend/pallas_call | solution.py:163
  177.3 2.4 %collective-permute-start.18 = (bf16[128,896]{1,0:T(8,128)(2,1)}, bf16[128,896]{1,0:T(8,128)(2,1)S(1)}, u32[]{:S(2)}, u32[]{:S(2)}) collective-permute-start(bf16[128,896]{1,0:T(8,128)(2,1)} %get-tuple-element.46), channel_id=1, source_target_pairs={{0,4},{2,6},{4,0},{6,2},{8,12},{10,14},{12,8},{14,10},{16,20},{18,... | collective-permute-start | bytes 688136 | tf_op jit(solution)/shard_map/ppermute | solution.py:243
  180.4 2.3 %collective-permute-start.19 = (bf16[128,896]{1,0:T(8,128)(2,1)}, bf16[128,896]{1,0:T(8,128)(2,1)S(1)}, u32[]{:S(2)}, u32[]{:S(2)}) collective-permute-start(bf16[128,896]{1,0:T(8,128)(2,1)} %get-tuple-element.47), channel_id=1, source_target_pairs={{0,6},{2,0},{4,2},{6,4},{8,14},{10,8},{12,10},{14,12},{16,22},{18,... | collective-permute-start | bytes 688136 | tf_op jit(solution)/shard_map/ppermute | solution.py:243
  185.2 4.7 %cache.1 = bf16[4,128,2,1792]{3,2,1,0:T(2,128)(2,1)} custom-call(s32[1]{0:T(128)} %bitcast.col_ref, s32[4]{0:T(128)S(1)} %dynamic-slice_subtract_fusion.slot_ref, bf16[3,2,128,896]{3,2,1,0:T(8,128)(2,1)S(1)} %copy-done.1, bf16[2,128,896]{2,1,0:T(8,128)(2,1)S(1)} %collective-permute-done.20.zlate_a, bf16[3,2,128,896]{3,2,1,0:T(8,128)(2,1)S(1)} %copy-done.3, ...), custom_call_target="tpu_custom_call" | custom-call | bytes 8388608 | tf_op jit(solution)/shard_map/cache/pallas_call | solution.py:222
  189.9 3.1 %unpack.1 = bf16[512,1792]{1,0:T(8,128)(2,1)} custom-call(s32[1]{0:T(128)} %bitcast.col_ref, bf16[128,896]{1,0:T(8,128)(2,1)S(1)} %copy-done.7, bf16[128,896]{1,0:T(8,128)(2,1)S(1)} %collective-permute-done.7.refs_1_, bf16[128,896]{1,0:T(8,128)(2,1)} %collective-permute-done.8.refs_2_, bf16[128,896]{1,0:T(8,128)(2,1)} %collective-permute-done.9.refs_3_, ...), custom_call_target="tpu_custom_call" | custom-call | bytes 4194304 | tf_op jit(solution)/shard_map/unpack/pallas_call | solution.py:196
  (94 shorter events, 20.5 us)
Async XLA Ops:
  6.6 36.0 %collective-permute-start.3 = (bf16[3,2,128,896]{3,2,1,0:T(8,128)(2,1)S(1)}, bf16[3,2,128,896]{3,2,1,0:T(8,128)(2,1)S(1)}, u32[]{:S(2)}, u32[]{:S(2)}) collective-permute-start(bf16[3,2,128,896]{3,2,1,0:T(8,128)(2,1)S(1)} %get-tuple-element.31), channel_id=1, source_target_pairs={{0,8},{2,10},{4,12},{6,14},{8,16},{10,18},{12,20},{14,22},{16,24},... | collective-permute-start | bytes 4128776 | tf_op jit(solution)/shard_map/ppermute | solution.py:246
  8.5 20.1 %collective-permute-start.1 = (bf16[3,128,896]{2,1,0:T(8,128)(2,1)}, bf16[3,128,896]{2,1,0:T(8,128)(2,1)S(1)}, u32[]{:S(2)}, u32[]{:S(2)}) collective-permute-start(bf16[3,128,896]{2,1,0:T(8,128)(2,1)} %get-tuple-element.29), channel_id=1, source_target_pairs={{0,4},{2,6},{4,0},{6,2},{8,12},{10,14},{12,8},{14,10},{16,20},{18,... | collective-permute-start | bytes 2064392 | tf_op jit(solution)/shard_map/ppermute | solution.py:243
  11.5 84.9 %collective-permute-start = (bf16[3,128,896]{2,1,0:T(8,128)(2,1)}, bf16[3,128,896]{2,1,0:T(8,128)(2,1)}, u32[]{:S(2)}, u32[]{:S(2)}) collective-permute-start(bf16[3,128,896]{2,1,0:T(8,128)(2,1)} %get-tuple-element.28), channel_id=1, source_target_pairs={{0,2},{2,4},{4,6},{6,0},{8,10},{10,12},{12,14},{14,8},{16,18},{18,... | collective-permute-start | bytes 2064392 | tf_op jit(solution)/shard_map/ppermute | solution.py:243
  12.1 84.4 %collective-permute-start.2 = (bf16[3,128,896]{2,1,0:T(8,128)(2,1)}, bf16[3,128,896]{2,1,0:T(8,128)(2,1)}, u32[]{:S(2)}, u32[]{:S(2)}) collective-permute-start(bf16[3,128,896]{2,1,0:T(8,128)(2,1)} %get-tuple-element.30), channel_id=1, source_target_pairs={{0,6},{2,0},{4,2},{6,4},{8,14},{10,8},{12,10},{14,12},{16,22},{18,... | collective-permute-start | bytes 2064392 | tf_op jit(solution)/shard_map/ppermute | solution.py:243
  51.9 91.6 %collective-permute-start.13 = (bf16[3,2,128,896]{3,2,1,0:T(8,128)(2,1)}, bf16[3,2,128,896]{3,2,1,0:T(8,128)(2,1)S(1)}, u32[]{:S(2)}, u32[]{:S(2)}) collective-permute-start(bf16[3,2,128,896]{3,2,1,0:T(8,128)(2,1)} %get-tuple-element.40), channel_id=1, source_target_pairs={{0,8},{2,10},{4,12},{6,14},{8,16},{10,18},{12,20},{14,22},{16,24},... | collective-permute-start | bytes 4128776 | tf_op jit(solution)/shard_map/ppermute | solution.py:246
  86.2 31.4 %copy-start.15 = (bf16[3,128,896]{2,1,0:T(8,128)(2,1)S(1)}, bf16[3,128,896]{2,1,0:T(8,128)(2,1)}, u32[]{:S(2)}) copy-start(bf16[3,128,896]{2,1,0:T(8,128)(2,1)} %copy-done.14) | copy-start | bytes 2064388
  86.2 39.2 %copy-start.13 = (bf16[3,128,896]{2,1,0:T(8,128)(2,1)S(1)}, bf16[3,128,896]{2,1,0:T(8,128)(2,1)}, u32[]{:S(2)}) copy-start(bf16[3,128,896]{2,1,0:T(8,128)(2,1)} %copy-done.12) | copy-start | bytes 2064388
  86.2 13.9 %collective-permute-start.5 = (bf16[2,128,896]{2,1,0:T(8,128)(2,1)S(1)}, bf16[2,128,896]{2,1,0:T(8,128)(2,1)S(1)}, u32[]{:S(2)}, u32[]{:S(2)}) collective-permute-start(bf16[2,128,896]{2,1,0:T(8,128)(2,1)S(1)} %slice.29), channel_id=1, source_target_pairs={{0,8},{2,10},{4,12},{6,14},{8,16},{10,18},{12,20},{14,22},{16,24},... | collective-permute-start | bytes 1376264 | tf_op jit(solution)/shard_map/ppermute | solution.py:246
  93.6 24.0 %collective-permute-start.6 = (bf16[2,128,896]{2,1,0:T(8,128)(2,1)S(1)}, bf16[2,128,896]{2,1,0:T(8,128)(2,1)S(1)}, u32[]{:S(2)}, u32[]{:S(2)}) collective-permute-start(bf16[2,128,896]{2,1,0:T(8,128)(2,1)S(1)} %get-tuple-element.54), channel_id=1, source_target_pairs={{0,6},{2,0},{4,2},{6,4},{8,14},{10,8},{12,10},{14,12},{16,22},{18,... | collective-permute-start | bytes 1376264 | tf_op jit(solution)/shard_map/ppermute | solution.py:243
  96.5 28.7 %collective-permute-start.4 = (bf16[2,128,896]{2,1,0:T(8,128)(2,1)S(1)}, bf16[2,128,896]{2,1,0:T(8,128)(2,1)S(1)}, u32[]{:S(2)}, u32[]{:S(2)}) collective-permute-start(bf16[2,128,896]{2,1,0:T(8,128)(2,1)S(1)} %get-tuple-element.55), channel_id=1, source_target_pairs={{0,2},{2,4},{4,6},{6,0},{8,10},{10,12},{12,14},{14,8},{16,18},{18,... | collective-permute-start | bytes 1376264 | tf_op jit(solution)/shard_map/ppermute | solution.py:243
  96.5 46.4 %collective-permute-start.11 = (bf16[3,128,896]{2,1,0:T(8,128)(2,1)S(1)}, bf16[3,128,896]{2,1,0:T(8,128)(2,1)S(1)}, u32[]{:S(2)}, u32[]{:S(2)}) collective-permute-start(bf16[3,128,896]{2,1,0:T(8,128)(2,1)S(1)} %copy-done.19), channel_id=1, source_target_pairs={{0,4},{2,6},{4,0},{6,2},{8,12},{10,14},{12,8},{14,10},{16,20},{18,... | collective-permute-start | bytes 2064392 | tf_op jit(solution)/shard_map/ppermute | solution.py:243
  100.1 46.8 %collective-permute-start.10 = (bf16[3,128,896]{2,1,0:T(8,128)(2,1)S(1)}, bf16[3,128,896]{2,1,0:T(8,128)(2,1)S(1)}, u32[]{:S(2)}, u32[]{:S(2)}) collective-permute-start(bf16[3,128,896]{2,1,0:T(8,128)(2,1)S(1)} %copy-done.17), channel_id=1, source_target_pairs={{0,2},{2,4},{4,6},{6,0},{8,10},{10,12},{12,14},{14,8},{16,18},{18,... | collective-permute-start | bytes 2064392 | tf_op jit(solution)/shard_map/ppermute | solution.py:243
  117.6 32.1 %collective-permute-start.12 = (bf16[3,128,896]{2,1,0:T(8,128)(2,1)S(1)}, bf16[3,128,896]{2,1,0:T(8,128)(2,1)S(1)}, u32[]{:S(2)}, u32[]{:S(2)}) collective-permute-start(bf16[3,128,896]{2,1,0:T(8,128)(2,1)S(1)} %copy-done.15), channel_id=1, source_target_pairs={{0,6},{2,0},{4,2},{6,4},{8,14},{10,8},{12,10},{14,12},{16,22},{18,... | collective-permute-start | bytes 2064392 | tf_op jit(solution)/shard_map/ppermute | solution.py:243
  143.0 12.4 %collective-permute-start.15 = (bf16[2,128,896]{2,1,0:T(8,128)(2,1)S(1)}, bf16[2,128,896]{2,1,0:T(8,128)(2,1)S(1)}, u32[]{:S(2)}, u32[]{:S(2)}) collective-permute-start(bf16[2,128,896]{2,1,0:T(8,128)(2,1)S(1)} %slice.32), channel_id=1, source_target_pairs={{0,8},{2,10},{4,12},{6,14},{8,16},{10,18},{12,20},{14,22},{16,24},... | collective-permute-start | bytes 1376264 | tf_op jit(solution)/shard_map/ppermute | solution.py:246
  143.6 11.7 %collective-permute-start.14 = (bf16[2,128,896]{2,1,0:T(8,128)(2,1)S(1)}, bf16[2,128,896]{2,1,0:T(8,128)(2,1)S(1)}, u32[]{:S(2)}, u32[]{:S(2)}) collective-permute-start(bf16[2,128,896]{2,1,0:T(8,128)(2,1)S(1)} %get-tuple-element.41), channel_id=1, source_target_pairs={{0,2},{2,4},{4,6},{6,0},{8,10},{10,12},{12,14},{14,8},{16,18},{18,... | collective-permute-start | bytes 1376264 | tf_op jit(solution)/shard_map/ppermute | solution.py:243
  143.7 12.5 %collective-permute-start.16 = (bf16[2,128,896]{2,1,0:T(8,128)(2,1)S(1)}, bf16[2,128,896]{2,1,0:T(8,128)(2,1)S(1)}, u32[]{:S(2)}, u32[]{:S(2)}) collective-permute-start(bf16[2,128,896]{2,1,0:T(8,128)(2,1)S(1)} %get-tuple-element.43), channel_id=1, source_target_pairs={{0,6},{2,0},{4,2},{6,4},{8,14},{10,8},{12,10},{14,12},{16,22},{18,... | collective-permute-start | bytes 1376264 | tf_op jit(solution)/shard_map/ppermute | solution.py:243
  146.9 30.4 %collective-permute-start.20 = (bf16[2,128,896]{2,1,0:T(8,128)(2,1)S(1)}, bf16[2,128,896]{2,1,0:T(8,128)(2,1)S(1)}, u32[]{:S(2)}, u32[]{:S(2)}) collective-permute-start(bf16[2,128,896]{2,1,0:T(8,128)(2,1)S(1)} %copy-done.21), channel_id=1, source_target_pairs={{0,8},{2,10},{4,12},{6,14},{8,16},{10,18},{12,20},{14,22},{16,24},... | collective-permute-start | bytes 1376264 | tf_op jit(solution)/shard_map/ppermute | solution.py:246
  149.7 30.0 %collective-permute-start.21 = (bf16[2,128,896]{2,1,0:T(8,128)(2,1)S(1)}, bf16[2,128,896]{2,1,0:T(8,128)(2,1)S(1)}, u32[]{:S(2)}, u32[]{:S(2)}) collective-permute-start(bf16[2,128,896]{2,1,0:T(8,128)(2,1)S(1)} %copy-done.23), channel_id=1, source_target_pairs={{0,8},{2,10},{4,12},{6,14},{8,16},{10,18},{12,20},{14,22},{16,24},... | collective-permute-start | bytes 1376264 | tf_op jit(solution)/shard_map/ppermute | solution.py:246
  155.3 21.2 %collective-permute-start.7 = (bf16[128,896]{1,0:T(8,128)(2,1)S(1)}, bf16[128,896]{1,0:T(8,128)(2,1)S(1)}, u32[]{:S(2)}, u32[]{:S(2)}) collective-permute-start(bf16[128,896]{1,0:T(8,128)(2,1)S(1)} %get-tuple-element.33), channel_id=1, source_target_pairs={{0,2},{2,4},{4,6},{6,0},{8,10},{10,12},{12,14},{14,8},{16,18},{18,... | collective-permute-start | bytes 688136 | tf_op jit(solution)/shard_map/ppermute | solution.py:243
  155.3 34.5 %collective-permute-start.8 = (bf16[128,896]{1,0:T(8,128)(2,1)}, bf16[128,896]{1,0:T(8,128)(2,1)}, u32[]{:S(2)}, u32[]{:S(2)}) collective-permute-start(bf16[128,896]{1,0:T(8,128)(2,1)} %get-tuple-element.34), channel_id=1, source_target_pairs={{0,4},{2,6},{4,0},{6,2},{8,12},{10,14},{12,8},{14,10},{16,20},{18,... | collective-permute-start | bytes 688136 | tf_op jit(solution)/shard_map/ppermute | solution.py:243
  156.2 33.6 %collective-permute-start.9 = (bf16[128,896]{1,0:T(8,128)(2,1)}, bf16[128,896]{1,0:T(8,128)(2,1)}, u32[]{:S(2)}, u32[]{:S(2)}) collective-permute-start(bf16[128,896]{1,0:T(8,128)(2,1)} %get-tuple-element.35), channel_id=1, source_target_pairs={{0,6},{2,0},{4,2},{6,4},{8,14},{10,8},{12,10},{14,12},{16,22},{18,... | collective-permute-start | bytes 688136 | tf_op jit(solution)/shard_map/ppermute | solution.py:243
  176.5 13.3 %collective-permute-start.17 = (bf16[128,896]{1,0:T(8,128)(2,1)}, bf16[128,896]{1,0:T(8,128)(2,1)S(1)}, u32[]{:S(2)}, u32[]{:S(2)}) collective-permute-start(bf16[128,896]{1,0:T(8,128)(2,1)} %get-tuple-element.45), channel_id=1, source_target_pairs={{0,2},{2,4},{4,6},{6,0},{8,10},{10,12},{12,14},{14,8},{16,18},{18,... | collective-permute-start | bytes 688136 | tf_op jit(solution)/shard_map/ppermute | solution.py:243
  177.3 12.5 %collective-permute-start.18 = (bf16[128,896]{1,0:T(8,128)(2,1)}, bf16[128,896]{1,0:T(8,128)(2,1)S(1)}, u32[]{:S(2)}, u32[]{:S(2)}) collective-permute-start(bf16[128,896]{1,0:T(8,128)(2,1)} %get-tuple-element.46), channel_id=1, source_target_pairs={{0,4},{2,6},{4,0},{6,2},{8,12},{10,14},{12,8},{14,10},{16,20},{18,... | collective-permute-start | bytes 688136 | tf_op jit(solution)/shard_map/ppermute | solution.py:243
  180.4 9.4 %collective-permute-start.19 = (bf16[128,896]{1,0:T(8,128)(2,1)}, bf16[128,896]{1,0:T(8,128)(2,1)S(1)}, u32[]{:S(2)}, u32[]{:S(2)}) collective-permute-start(bf16[128,896]{1,0:T(8,128)(2,1)} %get-tuple-element.47), channel_id=1, source_target_pairs={{0,6},{2,0},{4,2},{6,4},{8,14},{10,8},{12,10},{14,12},{16,22},{18,... | collective-permute-start | bytes 688136 | tf_op jit(solution)/shard_map/ppermute | solution.py:243
  (24 other events, 139.6 us)

commit v3 on v1

--- a/solution.py
+++ b/solution.py
@@ -244,6 +244,9 @@
     def ahead(value):
         return lax.ppermute(value, "blk", [(i, (i + COLS) % blocks) for i in range(blocks)])
 
+    def behind(value, *done):
+        return lax.optimization_barrier((value, *done))[0]
+
     row_seg = jnp.stack([segment_ids] + [across(segment_ids, r) for r in (1, 2, 3)])
     slots_here = jnp.broadcast_to(page_table[:, None], (pages, count // pages)).reshape(1, count)
     got = ahead(jnp.concatenate([row_seg, slots_here]))
@@ -260,21 +263,29 @@
     start_wide = jnp.broadcast_to(start[..., None], (COLS, count, 128))
 
     packed = [pack(col, queries, keys, values, half) for half in range(2)]
-    row, zrow, zlate, prior = [], [], [], []
+    pieces, late, zrows = [], [], []
+    first, turn = got, ()
+    attended = None
     for own, one, two, three, z_now, z_late in packed:
-        row.append((own, across(one, 1), across(two, 2), across(three, 3)))
-        zrow.append(ahead(z_now))
-    for half in range(2):
-        passed = ahead(row[half][2][1:])
-        prior.append((across(zrow[half][1], 1), passed, across(zrow[half][2], 3)))
-    for half in range(2):
-        zlate.append(ahead(packed[half][5]))
-    pieces = []
-    for half in range(2):
-        o0, o1, o2, o3 = attend(col, start_flat, start_wide, row[half], zrow[half], prior[half])
-        pieces += [o0, across(o1, 1), across(o2, 2), across(o3, 3)]
+        zrow = ahead(behind(z_now, first))
+        if turn:
+            one, three = behind(one, *turn), behind(three, *turn)
+            two = behind(two, first)
+        row = (own, across(one, 1), across(two, 2), across(three, 3))
+        zrow = behind(zrow, *row[1:])
+        from_z1, from_row, from_z3 = zrow[1], row[2][1:], zrow[2]
+        if attended is not None:
+            from_z1, from_row, from_z3 = (behind(x, attended) for x in (from_z1, from_row, from_z3))
+        prior = (across(from_z1, 1), ahead(from_row), across(from_z3, 3))
+        first, turn = zrow, (prior[0], prior[2])
+        outs = attend(col, start_flat, start_wide, row, zrow, prior)
+        attended = outs[0]
+        pieces += [outs[0]] + [across(outs[r], r) for r in (1, 2, 3)]
+        late.append(z_late)
+        zrows.append(zrow)
+    late = [ahead(behind(x, zrows[1])) for x in late]
     mixed = unpack(col, pieces)
-    kv = cache(col, slots, zrow[0], zlate[0], zrow[1], zlate[1])
+    kv = cache(col, slots, zrows[0], late[0], zrows[1], late[1])
     return (mixed, kv)
 
 

time: 202 us -> 173 us (0.86)
  the two profiles are of different devices: /device:TPU:72 before, /device:TPU:64 now
where the time goes in v3:
time: 173 us
  waiting for transfers between devices  59 us (34%)
  Pallas kernels  58.8 us (34%)
  starting transfers between devices  39.6 us (23%)
  local copies, waits for them, and re-layouts  14.9 us (9%)
    pallas_call x2, Pallas kernels, attend(): pl.pallas_call(attend_kernel, out_shape=[piece] * 4, in_specs=[SMEM, SMEM...  44.1 us
    ppermute x19, waiting for transfers between devices, across(): return lax.ppermute(value, 'blk', route)  42.2 us
    ppermute x19, starting transfers between devices, across(): return lax.ppermute(value, 'blk', route)  31.9 us
    ppermute x7, waiting for transfers between devices, ahead(): lax.ppermute(value, 'blk', [(i, (i + COLS) % blocks) for i in range(block...  16.7 us
    unnamed x53, local copies, waits for them, and re-layouts  11.9 us
    ppermute x7, starting transfers between devices, ahead(): lax.ppermute(value, 'blk', [(i, (i + COLS) % blocks) for i in range(block...  7.7 us
    pallas_call x2, Pallas kernels, pack(): pl.pallas_call(pack_kernel, grid=(1,), out_shape=[piece] * 4 + [jax.Shape...  6.96 us
    pallas_call x1, Pallas kernels, cache(): pl.pallas_call(cache_kernel, out_shape=jax.ShapeDtypeStruct((COLS, PAGE,...  4.61 us
  transfers between devices with their start and end apart: 26, of which 8 were waited for; matrix products, arithmetic and copies ran while one was open for 1% of the time, Pallas kernels for 32%

profile of v3, /device:TPU:64, one launch (start us, length us, event | category | flops | bytes accessed | tf_op | source)
XLA Modules:
  0.0 173.4 jit_solution(9128666745902529055)
XLA Ops:
  2.2 2.7 %collective-permute-start.1 = (s32[512]{0:T(512)}, s32[512]{0:T(512)S(1)}, u32[]{:S(2)}, u32[]{:S(2)}) collective-permute-start(s32[512]{0:T(512)} %param.8), channel_id=1, source_target_pairs={{0,4},{2,6},{4,0},{6,2},{8,12},{10,14},{12,8},{14,10},{16,20},{18,... | collective-permute-start | bytes 6152 | tf_op jit(solution)/shard_map/ppermute | solution.py:242
  10.2 2.0 %collective-permute-start.3 = (s32[5,512]{1,0:T(8,128)S(1)}, s32[5,512]{1,0:T(8,128)S(1)}, u32[]{:S(2)}, u32[]{:S(2)}) collective-permute-start(s32[5,512]{1,0:T(8,128)S(1)} %concatenate.4), channel_id=1, source_target_pairs={{0,8},{2,10},{4,12},{6,14},{8,16},{10,18},{12,20},{14,22},{16,24},... | collective-permute-start | bytes 30728 | tf_op jit(solution)/shard_map/ppermute | solution.py:245
  12.1 2.9 %pack.2 = (bf16[3,128,896]{2,1,0:T(8,128)(2,1)S(1)}, bf16[3,128,896]{2,1,0:T(8,128)(2,1)S(1)}, bf16[3,128,896]{2,1,0:T(8,128)(2,1)S(1)}, bf16[3,128,896]{2,1,0:T...) custom-call(s32[1]{0:T(128)} %bitcast.col_ref, bf16[512,1792]{1,0:T(8,128)(2,1)} %q_ref.3, ...), custom_call_target="tpu_custom_call" | custom-call | bytes 6291456 | tf_op jit(solution)/shard_map/pack/pallas_call | solution.py:55
  16.7 3.1 %collective-permute-start.7 = (bf16[3,2,128,896]{3,2,1,0:T(8,128)(2,1)S(1)}, bf16[3,2,128,896]{3,2,1,0:T(8,128)(2,1)S(1)}, u32[]{:S(2)}, u32[]{:S(2)}) collective-permute-start(bf16[3,2,128,896]{3,2,1,0:T(8,128)(2,1)S(1)} %get-tuple-element.39), channel_id=1, source_target_pairs={{0,8},{2,10},{4,12},{6,14},{8,16},{10,18},{12,20},{14,22},{16,24},... | collective-permute-start | bytes 4128776 | tf_op jit(solution)/shard_map/ppermute | solution.py:245
  20.1 3.8 %collective-permute-start.5 = (bf16[3,128,896]{2,1,0:T(8,128)(2,1)S(1)}, bf16[3,128,896]{2,1,0:T(8,128)(2,1)S(1)}, u32[]{:S(2)}, u32[]{:S(2)}) collective-permute-start(bf16[3,128,896]{2,1,0:T(8,128)(2,1)S(1)} %get-tuple-element.36), channel_id=1, source_target_pairs={{0,4},{2,6},{4,0},{6,2},{8,12},{10,14},{12,8},{14,10},{16,20},{18,... | collective-permute-start | bytes 2064392 | tf_op jit(solution)/shard_map/ppermute | solution.py:242
  24.0 4.0 %pack.3 = (bf16[3,128,896]{2,1,0:T(8,128)(2,1)S(1)}, bf16[3,128,896]{2,1,0:T(8,128)(2,1)S(1)}, bf16[3,128,896]{2,1,0:T(8,128)(2,1)S(1)}, bf16[3,128,896]{2,1,0:T...) custom-call(s32[1]{0:T(128)} %bitcast.col_ref, bf16[512,1792]{1,0:T(8,128)(2,1)} %q_ref.3, ...), custom_call_target="tpu_custom_call" | custom-call | bytes 6291456 | tf_op jit(solution)/shard_map/pack/pallas_call | solution.py:55
  32.3 6.9 %collective-permute-done.4.a1 = bf16[3,128,896]{2,1,0:T(8,128)(2,1)S(1)} collective-permute-done((bf16[3,128,896]{2,1,0:T(8,128)(2,1)S(1)}, bf16[3,128,896]{2,1,0:T(8,128)(2,1)S(1)}, u32[]{:S(2)}, u32[]{:S(2)}) %collective-permute-start.4) | collective-permute-done | bytes 688160 | tf_op jit(solution)/shard_map/ppermute | solution.py:242
  40.0 11.6 %collective-permute-done.5.a2 = bf16[3,128,896]{2,1,0:T(8,128)(2,1)S(1)} collective-permute-done((bf16[3,128,896]{2,1,0:T(8,128)(2,1)S(1)}, bf16[3,128,896]{2,1,0:T(8,128)(2,1)S(1)}, u32[]{:S(2)}, u32[]{:S(2)}) %collective-permute-start.5) | collective-permute-done | bytes 688160 | tf_op jit(solution)/shard_map/ppermute | solution.py:242
  55.4 2.4 %collective-permute-start.10 = (bf16[2,128,896]{2,1,0:T(8,128)(2,1)}, bf16[2,128,896]{2,1,0:T(8,128)(2,1)}, u32[]{:S(2)}, u32[]{:S(2)}) collective-permute-start(bf16[2,128,896]{2,1,0:T(8,128)(2,1)} %get-tuple-element.68), channel_id=1, source_target_pairs={{0,6},{2,0},{4,2},{6,4},{8,14},{10,8},{12,10},{14,12},{16,22},{18,... | collective-permute-start | bytes 1376264 | tf_op jit(solution)/shard_map/ppermute | solution.py:242
  59.9 8.1 %collective-permute-done.8.p1 = bf16[2,128,896]{2,1,0:T(8,128)(2,1)} collective-permute-done((bf16[2,128,896]{2,1,0:T(8,128)(2,1)}, bf16[2,128,896]{2,1,0:T(8,128)(2,1)}, u32[]{:S(2)}, u32[]{:S(2)}) %collective-permute-start.8) | collective-permute-done | bytes 458784 | tf_op jit(solution)/shard_map/ppermute | solution.py:242
  68.0 13.3 %collective-permute-done.10.p3 = bf16[2,128,896]{2,1,0:T(8,128)(2,1)} collective-permute-done((bf16[2,128,896]{2,1,0:T(8,128)(2,1)}, bf16[2,128,896]{2,1,0:T(8,128)(2,1)}, u32[]{:S(2)}, u32[]{:S(2)}) %collective-permute-start.10) | collective-permute-done | bytes 458784 | tf_op jit(solution)/shard_map/ppermute | solution.py:242
  81.2 4.2 %collective-permute-start.16 = (bf16[3,128,896]{2,1,0:T(8,128)(2,1)}, bf16[3,128,896]{2,1,0:T(8,128)(2,1)S(1)}, u32[]{:S(2)}, u32[]{:S(2)}) collective-permute-start(bf16[3,128,896]{2,1,0:T(8,128)(2,1)} %copy-done.14), channel_id=1, source_target_pairs={{0,6},{2,0},{4,2},{6,4},{8,14},{10,8},{12,10},{14,12},{16,22},{18,... | collective-permute-start | bytes 2064392 | tf_op jit(solution)/shard_map/ppermute | solution.py:242
  85.7 7.9 %collective-permute-done.9.p2 = bf16[2,128,896]{2,1,0:T(8,128)(2,1)S(1)} collective-permute-done((bf16[2,128,896]{2,1,0:T(8,128)(2,1)S(1)}, bf16[2,128,896]{2,1,0:T(8,128)(2,1)S(1)}, u32[]{:S(2)}, u32[]{:S(2)}) %collective-permute-start.9) | collective-permute-done | bytes 458784 | tf_op jit(solution)/shard_map/ppermute | solution.py:245
  93.9 22.1 %attend.2 = (bf16[128,896]{1,0:T(8,128)(2,1)S(1)}, bf16[128,896]{1,0:T(8,128)(2,1)S(1)}, bf16[128,896]{1,0:T(8,128)(2,1)}, bf16[128,896]{1,0:T(8,128)(2,1)}) custom-call(s32[1]{0:T(128)} %bitcast.col_ref, s32[2048]{0:T(1024)S(1)} %bitcast.18, s32[4,512,128]{2,1,0:T(8,128)S(1)} %broadcast_in_dim.34.start_ref, bf16[3,128,896]{2,1,0:T(8,128)(2,1)S(1)} %copy-done.13, ...), custom_call_target="tpu_custom_call" | custom-call | flops 4294967296 | bytes 6291456 | tf_op jit(solution)/shard_map/attend/pallas_call | solution.py:162
  116.7 1.9 %collective-permute-start.18 = (bf16[2,128,896]{2,1,0:T(8,128)(2,1)S(1)}, bf16[2,128,896]{2,1,0:T(8,128)(2,1)S(1)}, u32[]{:S(2)}, u32[]{:S(2)}) collective-permute-start(bf16[2,128,896]{2,1,0:T(8,128)(2,1)S(1)} %get-tuple-element.55), channel_id=1, source_target_pairs={{0,2},{2,4},{4,6},{6,0},{8,10},{10,12},{12,14},{14,8},{16,18},{18,... | collective-permute-start | bytes 1376264 | tf_op jit(solution)/shard_map/ppermute | solution.py:242
  118.6 1.8 %collective-permute-start.20 = (bf16[2,128,896]{2,1,0:T(8,128)(2,1)S(1)}, bf16[2,128,896]{2,1,0:T(8,128)(2,1)S(1)}, u32[]{:S(2)}, u32[]{:S(2)}) collective-permute-start(bf16[2,128,896]{2,1,0:T(8,128)(2,1)S(1)} %get-tuple-element.57), channel_id=1, source_target_pairs={{0,6},{2,0},{4,2},{6,4},{8,14},{10,8},{12,10},{14,12},{16,22},{18,... | collective-permute-start | bytes 1376264 | tf_op jit(solution)/shard_map/ppermute | solution.py:242
  120.8 8.8 %collective-permute-done.19.p2 = bf16[2,128,896]{2,1,0:T(8,128)(2,1)S(1)} collective-permute-done((bf16[2,128,896]{2,1,0:T(8,128)(2,1)S(1)}, bf16[2,128,896]{2,1,0:T(8,128)(2,1)S(1)}, u32[]{:S(2)}, u32[]{:S(2)}) %collective-permute-start.19) | collective-permute-done | bytes 458784 | tf_op jit(solution)/shard_map/ppermute | solution.py:245
  129.6 1.9 %collective-permute-start.11 = (bf16[128,896]{1,0:T(8,128)(2,1)S(1)}, bf16[128,896]{1,0:T(8,128)(2,1)S(1)}, u32[]{:S(2)}, u32[]{:S(2)}) collective-permute-start(bf16[128,896]{1,0:T(8,128)(2,1)S(1)} %get-tuple-element.42), channel_id=1, source_target_pairs={{0,2},{2,4},{4,6},{6,0},{8,10},{10,12},{12,14},{14,8},{16,18},{18,... | collective-permute-start | bytes 688136 | tf_op jit(solution)/shard_map/ppermute | solution.py:242
  131.6 3.2 %collective-permute-start.12 = (bf16[128,896]{1,0:T(8,128)(2,1)}, bf16[128,896]{1,0:T(8,128)(2,1)}, u32[]{:S(2)}, u32[]{:S(2)}) collective-permute-start(bf16[128,896]{1,0:T(8,128)(2,1)} %get-tuple-element.43), channel_id=1, source_target_pairs={{0,4},{2,6},{4,0},{6,2},{8,12},{10,14},{12,8},{14,10},{16,20},{18,... | collective-permute-start | bytes 688136 | tf_op jit(solution)/shard_map/ppermute | solution.py:242
  134.8 22.0 %attend.3 = (bf16[128,896]{1,0:T(8,128)(2,1)S(1)}, bf16[128,896]{1,0:T(8,128)(2,1)}, bf16[128,896]{1,0:T(8,128)(2,1)}, bf16[128,896]{1,0:T(8,128)(2,1)}) custom-call(s32[1]{0:T(128)} %bitcast.col_ref, s32[2048]{0:T(1024)S(1)} %bitcast.19, s32[4,512,128]{2,1,0:T(8,128)S(1)} %broadcast_in_dim.34.start_ref, bf16[3,128,896]{2,1,0:T(8,128)(2,1)S(1)} %copy-done.11, ...), custom_call_target="tpu_custom_call" | custom-call | flops 4294967296 | bytes 6291456 | tf_op jit(solution)/shard_map/attend/pallas_call | solution.py:162
  157.6 2.0 %collective-permute-start.21 = (bf16[128,896]{1,0:T(8,128)(2,1)}, bf16[128,896]{1,0:T(8,128)(2,1)S(1)}, u32[]{:S(2)}, u32[]{:S(2)}) collective-permute-start(bf16[128,896]{1,0:T(8,128)(2,1)} %get-tuple-element.59), channel_id=1, source_target_pairs={{0,2},{2,4},{4,6},{6,0},{8,10},{10,12},{12,14},{14,8},{16,18},{18,... | collective-permute-start | bytes 688136 | tf_op jit(solution)/shard_map/ppermute | solution.py:242
  160.7 2.5 %collective-permute-start.23 = (bf16[128,896]{1,0:T(8,128)(2,1)}, bf16[128,896]{1,0:T(8,128)(2,1)S(1)}, u32[]{:S(2)}, u32[]{:S(2)}) collective-permute-start(bf16[128,896]{1,0:T(8,128)(2,1)} %get-tuple-element.61), channel_id=1, source_target_pairs={{0,6},{2,0},{4,2},{6,4},{8,14},{10,8},{12,10},{14,12},{16,22},{18,... | collective-permute-start | bytes 688136 | tf_op jit(solution)/shard_map/ppermute | solution.py:242
  165.6 4.6 %cache.1 = bf16[4,128,2,1792]{3,2,1,0:T(2,128)(2,1)} custom-call(s32[1]{0:T(128)} %bitcast.col_ref, s32[4]{0:T(128)S(1)} %subtract_bitcast_fusion.slot_ref, bf16[3,2,128,896]{3,2,1,0:T(8,128)(2,1)S(1)} %copy-done.1, bf16[2,128,896]{2,1,0:T(8,128)(2,1)S(1)} %collective-permute-done.24.zlate_a, bf16[3,2,128,896]{3,2,1,0:T(8,128)(2,1)S(1)} %copy-done.3, ...), custom_call_target="tpu_custom_call" | custom-call | bytes 8388608 | tf_op jit(solution)/shard_map/cache/pallas_call | solution.py:221
  170.3 3.1 %unpack.1 = bf16[512,1792]{1,0:T(8,128)(2,1)} custom-call(s32[1]{0:T(128)} %bitcast.col_ref, bf16[128,896]{1,0:T(8,128)(2,1)S(1)} %copy-done.7, bf16[128,896]{1,0:T(8,128)(2,1)S(1)} %collective-permute-done.11.refs_1_, bf16[128,896]{1,0:T(8,128)(2,1)} %collective-permute-done.12.refs_2_, bf16[128,896]{1,0:T(8,128)(2,1)} %collective-permute-done.13.refs_3_, ...), custom_call_target="tpu_custom_call" | custom-call | bytes 4194304 | tf_op jit(solution)/shard_map/unpack/pallas_call | solution.py:195
  (100 shorter events, 25.6 us)
Async XLA Ops:
  0.6 5.7 %collective-permute-start = (s32[512]{0:T(512)}, s32[512]{0:T(512)S(1)}, u32[]{:S(2)}, u32[]{:S(2)}) collective-permute-start(s32[512]{0:T(512)} %param.8), channel_id=1, source_target_pairs={{0,2},{2,4},{4,6},{6,0},{8,10},{10,12},{12,14},{14,8},{16,18},{18,... | collective-permute-start | bytes 6152 | tf_op jit(solution)/shard_map/ppermute | solution.py:242
  10.2 6.5 %collective-permute-start.3 = (s32[5,512]{1,0:T(8,128)S(1)}, s32[5,512]{1,0:T(8,128)S(1)}, u32[]{:S(2)}, u32[]{:S(2)}) collective-permute-start(s32[5,512]{1,0:T(8,128)S(1)} %concatenate.4), channel_id=1, source_target_pairs={{0,8},{2,10},{4,12},{6,14},{8,16},{10,18},{12,20},{14,22},{16,24},... | collective-permute-start | bytes 30728 | tf_op jit(solution)/shard_map/ppermute | solution.py:245
  16.7 35.8 %collective-permute-start.7 = (bf16[3,2,128,896]{3,2,1,0:T(8,128)(2,1)S(1)}, bf16[3,2,128,896]{3,2,1,0:T(8,128)(2,1)S(1)}, u32[]{:S(2)}, u32[]{:S(2)}) collective-permute-start(bf16[3,2,128,896]{3,2,1,0:T(8,128)(2,1)S(1)} %get-tuple-element.39), channel_id=1, source_target_pairs={{0,8},{2,10},{4,12},{6,14},{8,16},{10,18},{12,20},{14,22},{16,24},... | collective-permute-start | bytes 4128776 | tf_op jit(solution)/shard_map/ppermute | solution.py:245
  19.8 19.3 %collective-permute-start.4 = (bf16[3,128,896]{2,1,0:T(8,128)(2,1)S(1)}, bf16[3,128,896]{2,1,0:T(8,128)(2,1)S(1)}, u32[]{:S(2)}, u32[]{:S(2)}) collective-permute-start(bf16[3,128,896]{2,1,0:T(8,128)(2,1)S(1)} %get-tuple-element.35), channel_id=1, source_target_pairs={{0,2},{2,4},{4,6},{6,0},{8,10},{10,12},{12,14},{14,8},{16,18},{18,... | collective-permute-start | bytes 2064392 | tf_op jit(solution)/shard_map/ppermute | solution.py:242
  20.1 31.5 %collective-permute-start.5 = (bf16[3,128,896]{2,1,0:T(8,128)(2,1)S(1)}, bf16[3,128,896]{2,1,0:T(8,128)(2,1)S(1)}, u32[]{:S(2)}, u32[]{:S(2)}) collective-permute-start(bf16[3,128,896]{2,1,0:T(8,128)(2,1)S(1)} %get-tuple-element.36), channel_id=1, source_target_pairs={{0,4},{2,6},{4,0},{6,2},{8,12},{10,14},{12,8},{14,10},{16,20},{18,... | collective-permute-start | bytes 2064392 | tf_op jit(solution)/shard_map/ppermute | solution.py:242
  23.9 27.7 %collective-permute-start.6 = (bf16[3,128,896]{2,1,0:T(8,128)(2,1)S(1)}, bf16[3,128,896]{2,1,0:T(8,128)(2,1)S(1)}, u32[]{:S(2)}, u32[]{:S(2)}) collective-permute-start(bf16[3,128,896]{2,1,0:T(8,128)(2,1)S(1)} %get-tuple-element.37), channel_id=1, source_target_pairs={{0,6},{2,0},{4,2},{6,4},{8,14},{10,8},{12,10},{14,12},{16,22},{18,... | collective-permute-start | bytes 2064392 | tf_op jit(solution)/shard_map/ppermute | solution.py:242
  52.5 63.7 %collective-permute-start.17 = (bf16[3,2,128,896]{3,2,1,0:T(8,128)(2,1)}, bf16[3,2,128,896]{3,2,1,0:T(8,128)(2,1)S(1)}, u32[]{:S(2)}, u32[]{:S(2)}) collective-permute-start(bf16[3,2,128,896]{3,2,1,0:T(8,128)(2,1)} %get-tuple-element.53), channel_id=1, source_target_pairs={{0,8},{2,10},{4,12},{6,14},{8,16},{10,18},{12,20},{14,22},{16,24},... | collective-permute-start | bytes 4128776 | tf_op jit(solution)/shard_map/ppermute | solution.py:245
  54.5 13.4 %collective-permute-start.8 = (bf16[2,128,896]{2,1,0:T(8,128)(2,1)}, bf16[2,128,896]{2,1,0:T(8,128)(2,1)}, u32[]{:S(2)}, u32[]{:S(2)}) collective-permute-start(bf16[2,128,896]{2,1,0:T(8,128)(2,1)} %get-tuple-element.69), channel_id=1, source_target_pairs={{0,2},{2,4},{4,6},{6,0},{8,10},{10,12},{12,14},{14,8},{16,18},{18,... | collective-permute-start | bytes 1376264 | tf_op jit(solution)/shard_map/ppermute | solution.py:242
  55.4 25.9 %collective-permute-start.10 = (bf16[2,128,896]{2,1,0:T(8,128)(2,1)}, bf16[2,128,896]{2,1,0:T(8,128)(2,1)}, u32[]{:S(2)}, u32[]{:S(2)}) collective-permute-start(bf16[2,128,896]{2,1,0:T(8,128)(2,1)} %get-tuple-element.68), channel_id=1, source_target_pairs={{0,6},{2,0},{4,2},{6,4},{8,14},{10,8},{12,10},{14,12},{16,22},{18,... | collective-permute-start | bytes 1376264 | tf_op jit(solution)/shard_map/ppermute | solution.py:242
  57.8 35.7 %collective-permute-start.9 = (bf16[2,128,896]{2,1,0:T(8,128)(2,1)S(1)}, bf16[2,128,896]{2,1,0:T(8,128)(2,1)S(1)}, u32[]{:S(2)}, u32[]{:S(2)}) collective-permute-start(bf16[2,128,896]{2,1,0:T(8,128)(2,1)S(1)} %slice.33), channel_id=1, source_target_pairs={{0,8},{2,10},{4,12},{6,14},{8,16},{10,18},{12,20},{14,22},{16,24},... | collective-permute-start | bytes 1376264 | tf_op jit(solution)/shard_map/ppermute | solution.py:245
  58.9 57.1 %collective-permute-start.15 = (bf16[3,128,896]{2,1,0:T(8,128)(2,1)}, bf16[3,128,896]{2,1,0:T(8,128)(2,1)S(1)}, u32[]{:S(2)}, u32[]{:S(2)}) collective-permute-start(bf16[3,128,896]{2,1,0:T(8,128)(2,1)} %copy-done.18), channel_id=1, source_target_pairs={{0,4},{2,6},{4,0},{6,2},{8,12},{10,14},{12,8},{14,10},{16,20},{18,... | collective-permute-start | bytes 2064392 | tf_op jit(solution)/shard_map/ppermute | solution.py:242
  81.2 35.0 %collective-permute-start.14 = (bf16[3,128,896]{2,1,0:T(8,128)(2,1)}, bf16[3,128,896]{2,1,0:T(8,128)(2,1)S(1)}, u32[]{:S(2)}, u32[]{:S(2)}) collective-permute-start(bf16[3,128,896]{2,1,0:T(8,128)(2,1)} %copy-done.15), channel_id=1, source_target_pairs={{0,2},{2,4},{4,6},{6,0},{8,10},{10,12},{12,14},{14,8},{16,18},{18,... | collective-permute-start | bytes 2064392 | tf_op jit(solution)/shard_map/ppermute | solution.py:242
  81.2 35.0 %collective-permute-start.16 = (bf16[3,128,896]{2,1,0:T(8,128)(2,1)}, bf16[3,128,896]{2,1,0:T(8,128)(2,1)S(1)}, u32[]{:S(2)}, u32[]{:S(2)}) collective-permute-start(bf16[3,128,896]{2,1,0:T(8,128)(2,1)} %copy-done.14), channel_id=1, source_target_pairs={{0,6},{2,0},{4,2},{6,4},{8,14},{10,8},{12,10},{14,12},{16,22},{18,... | collective-permute-start | bytes 2064392 | tf_op jit(solution)/shard_map/ppermute | solution.py:242
  116.1 13.5 %collective-permute-start.19 = (bf16[2,128,896]{2,1,0:T(8,128)(2,1)S(1)}, bf16[2,128,896]{2,1,0:T(8,128)(2,1)S(1)}, u32[]{:S(2)}, u32[]{:S(2)}) collective-permute-start(bf16[2,128,896]{2,1,0:T(8,128)(2,1)S(1)} %slice.34), channel_id=1, source_target_pairs={{0,8},{2,10},{4,12},{6,14},{8,16},{10,18},{12,20},{14,22},{16,24},... | collective-permute-start | bytes 1376264 | tf_op jit(solution)/shard_map/ppermute | solution.py:245
  116.7 14.8 %collective-permute-start.18 = (bf16[2,128,896]{2,1,0:T(8,128)(2,1)S(1)}, bf16[2,128,896]{2,1,0:T(8,128)(2,1)S(1)}, u32[]{:S(2)}, u32[]{:S(2)}) collective-permute-start(bf16[2,128,896]{2,1,0:T(8,128)(2,1)S(1)} %get-tuple-element.55), channel_id=1, source_target_pairs={{0,2},{2,4},{4,6},{6,0},{8,10},{10,12},{12,14},{14,8},{16,18},{18,... | collective-permute-start | bytes 1376264 | tf_op jit(solution)/shard_map/ppermute | solution.py:242
  118.6 16.2 %collective-permute-start.20 = (bf16[2,128,896]{2,1,0:T(8,128)(2,1)S(1)}, bf16[2,128,896]{2,1,0:T(8,128)(2,1)S(1)}, u32[]{:S(2)}, u32[]{:S(2)}) collective-permute-start(bf16[2,128,896]{2,1,0:T(8,128)(2,1)S(1)} %get-tuple-element.57), channel_id=1, source_target_pairs={{0,6},{2,0},{4,2},{6,4},{8,14},{10,8},{12,10},{14,12},{16,22},{18,... | collective-permute-start | bytes 1376264 | tf_op jit(solution)/shard_map/ppermute | solution.py:242
  120.4 39.2 %collective-permute-start.24 = (bf16[2,128,896]{2,1,0:T(8,128)(2,1)S(1)}, bf16[2,128,896]{2,1,0:T(8,128)(2,1)S(1)}, u32[]{:S(2)}, u32[]{:S(2)}) collective-permute-start(bf16[2,128,896]{2,1,0:T(8,128)(2,1)S(1)} %copy-done.22), channel_id=1, source_target_pairs={{0,8},{2,10},{4,12},{6,14},{8,16},{10,18},{12,20},{14,22},{16,24},... | collective-permute-start | bytes 1376264 | tf_op jit(solution)/shard_map/ppermute | solution.py:245
  120.4 39.5 %collective-permute-start.25 = (bf16[2,128,896]{2,1,0:T(8,128)(2,1)S(1)}, bf16[2,128,896]{2,1,0:T(8,128)(2,1)S(1)}, u32[]{:S(2)}, u32[]{:S(2)}) collective-permute-start(bf16[2,128,896]{2,1,0:T(8,128)(2,1)S(1)} %copy-done.24), channel_id=1, source_target_pairs={{0,8},{2,10},{4,12},{6,14},{8,16},{10,18},{12,20},{14,22},{16,24},... | collective-permute-start | bytes 1376264 | tf_op jit(solution)/shard_map/ppermute | solution.py:245
  129.6 27.9 %collective-permute-start.11 = (bf16[128,896]{1,0:T(8,128)(2,1)S(1)}, bf16[128,896]{1,0:T(8,128)(2,1)S(1)}, u32[]{:S(2)}, u32[]{:S(2)}) collective-permute-start(bf16[128,896]{1,0:T(8,128)(2,1)S(1)} %get-tuple-element.42), channel_id=1, source_target_pairs={{0,2},{2,4},{4,6},{6,0},{8,10},{10,12},{12,14},{14,8},{16,18},{18,... | collective-permute-start | bytes 688136 | tf_op jit(solution)/shard_map/ppermute | solution.py:242
  131.6 38.6 %collective-permute-start.12 = (bf16[128,896]{1,0:T(8,128)(2,1)}, bf16[128,896]{1,0:T(8,128)(2,1)}, u32[]{:S(2)}, u32[]{:S(2)}) collective-permute-start(bf16[128,896]{1,0:T(8,128)(2,1)} %get-tuple-element.43), channel_id=1, source_target_pairs={{0,4},{2,6},{4,0},{6,2},{8,12},{10,14},{12,8},{14,10},{16,20},{18,... | collective-permute-start | bytes 688136 | tf_op jit(solution)/shard_map/ppermute | solution.py:242
  134.8 35.4 %collective-permute-start.13 = (bf16[128,896]{1,0:T(8,128)(2,1)}, bf16[128,896]{1,0:T(8,128)(2,1)}, u32[]{:S(2)}, u32[]{:S(2)}) collective-permute-start(bf16[128,896]{1,0:T(8,128)(2,1)} %get-tuple-element.44), channel_id=1, source_target_pairs={{0,6},{2,0},{4,2},{6,4},{8,14},{10,8},{12,10},{14,12},{16,22},{18,... | collective-permute-start | bytes 688136 | tf_op jit(solution)/shard_map/ppermute | solution.py:242
  157.6 12.6 %collective-permute-start.21 = (bf16[128,896]{1,0:T(8,128)(2,1)}, bf16[128,896]{1,0:T(8,128)(2,1)S(1)}, u32[]{:S(2)}, u32[]{:S(2)}) collective-permute-start(bf16[128,896]{1,0:T(8,128)(2,1)} %get-tuple-element.59), channel_id=1, source_target_pairs={{0,2},{2,4},{4,6},{6,0},{8,10},{10,12},{12,14},{14,8},{16,18},{18,... | collective-permute-start | bytes 688136 | tf_op jit(solution)/shard_map/ppermute | solution.py:242
  159.6 10.6 %collective-permute-start.22 = (bf16[128,896]{1,0:T(8,128)(2,1)}, bf16[128,896]{1,0:T(8,128)(2,1)S(1)}, u32[]{:S(2)}, u32[]{:S(2)}) collective-permute-start(bf16[128,896]{1,0:T(8,128)(2,1)} %get-tuple-element.60), channel_id=1, source_target_pairs={{0,4},{2,6},{4,0},{6,2},{8,12},{10,14},{12,8},{14,10},{16,20},{18,... | collective-permute-start | bytes 688136 | tf_op jit(solution)/shard_map/ppermute | solution.py:242
  160.7 9.6 %collective-permute-start.23 = (bf16[128,896]{1,0:T(8,128)(2,1)}, bf16[128,896]{1,0:T(8,128)(2,1)S(1)}, u32[]{:S(2)}, u32[]{:S(2)}) collective-permute-start(bf16[128,896]{1,0:T(8,128)(2,1)} %get-tuple-element.61), channel_id=1, source_target_pairs={{0,6},{2,0},{4,2},{6,4},{8,14},{10,8},{12,10},{14,12},{16,22},{18,... | collective-permute-start | bytes 688136 | tf_op jit(solution)/shard_map/ppermute | solution.py:242
  (28 other events, 225.3 us)
